TPU v7x, 256 devices: a whole 4x4x8 slice. The times are simulated.
256 devices in a mesh: chan: 64 (over z, x, core), tile: 4 (over y).
Axes of the slice: x: 4, y: 4, z: 8, core: 2. Of those that a mesh axis runs over, the one named last changes fastest.
Arguments:
- gamma_pair: bfloat16 [64, 2048, 2048], P('chan', 'tile'), may hold values from -8 to 8, as said below
- energies: float32 [64, 2048], P('chan'), may hold values from 0.5 to 4
- occupancy: int32 [64, 2048], P('chan'), may hold values from 0 to 2
- recoup: bfloat16 [8, 128, 128], replicated, may hold values from -0.5 to 0.5
- recoup_class: int32 [64, 16, 16], P('chan', 'tile'), may hold values from 0 to 7
- send_slot: int32 [64, 16, 16], P('chan', 'tile'), may hold values from 0 to 63, as said below
- recv_slot: int32 [64, 16, 16], P('chan', 'tile'), may hold values from 0 to 63, as said below
Outputs:
- flowed: float32 [64, 2048, 2048], P('chan', 'tile')
Inputs may be any that keep to these rules, and one draw needn't show every extreme that they name: gamma_pair is symmetric in its last two dimensions. `send_slot`: for each channel and block b, the 64 entries of tile rows b * 4 to (b + 1) * 4 - 1 are a permutation of 0 to 63; entry q = 1 * c + s with 0 <= s < 1 sends the tile to channel c in its slot s, so each channel receives exactly 1 tiles from each block of each channel. `recv_slot`: for each channel and block b, the 64 entries of tile rows b * 4 to (b + 1) * 4 - 1 are a permutation of 0 to 63; entry q = 1 * c + s with 0 <= s < 1 names the tile received from channel c in its slot s.
All inputs are finite; a program needn't handle non-finite values.
Results may differ from a plain program's by a relative error of at most 0.002.
Values may be sent and summed in bfloat16 or wider, within the bound.
No kernel may reach another device: no remote copies, remote signals or barrier semaphores. Data moves between devices by JAX's collectives and lax.ppermute only.
A program may use at most 128 MiB of HBM per device.

v0:
```python
import math

import jax
import jax.numpy as jnp
from jax import lax
from jax.sharding import PartitionSpec as P


def split_tiles(matrix, tile_size):
    row_count = matrix.shape[1]
    full_width = matrix.shape[2]
    blocks = matrix.reshape(row_count // tile_size, tile_size, full_width // tile_size, tile_size)
    return jnp.transpose(blocks, (0, 2, 1, 3)).reshape(-1, tile_size, tile_size)


def join_tiles(tile_set, row_count, full_width):
    tile_size = tile_set.shape[1]
    blocks = tile_set.reshape(row_count // tile_size, full_width // tile_size, tile_size, tile_size)
    return jnp.transpose(blocks, (0, 2, 1, 3)).reshape(1, row_count, full_width)


def on_device(gamma_pair, energies, occupancy, recoup, recoup_class, send_slot, recv_slot):
    row_count = gamma_pair.shape[1]
    full_width = gamma_pair.shape[2]
    tile_size = recoup.shape[1]
    first_row = lax.axis_index("tile") * row_count
    occ_float = occupancy[0].astype(jnp.float32)
    energy_all = energies[0]
    occ_rows = lax.dynamic_slice_in_dim(occ_float, first_row, row_count)
    energy_rows = lax.dynamic_slice_in_dim(energy_all, first_row, row_count)
    upper_mask = ((occ_rows[:, None] == 0.0) & (occ_float[None, :] == 2.0)).astype(jnp.float32)
    lower_mask = ((occ_rows[:, None] == 2.0) & (occ_float[None, :] == 0.0)).astype(jnp.float32)
    denom = energy_rows[:, None] + energy_all[None, :]
    eta_local = (gamma_pair[0].astype(jnp.float32) * (upper_mask - lower_mask) / denom).astype(
        jnp.bfloat16
    )[None]
    weight_p = (1.0 - occ_float).astype(jnp.bfloat16)
    eta_scaled = eta_local * weight_p[None, None, :]
    columns = eta_scaled
    ladder_half = jnp.einsum(
        "crk,ckn->crn",
        columns,
        lax.all_gather(gamma_pair, "tile", axis=1, tiled=True),
        preferred_element_type=jnp.float32,
    )
    gamma_scaled = gamma_pair * weight_p[None, None, :]
    ladder_mirror = jnp.einsum(
        "crk,cnk->crn",
        gamma_scaled,
        lax.all_gather(eta_local, "tile", axis=1, tiled=True),
        preferred_element_type=jnp.float32,
    )
    ladder = ladder_half + ladder_mirror
    class_flat = recoup_class.reshape(-1)
    picker = (class_flat[:, None] == jnp.arange(recoup.shape[0], dtype=jnp.int32)[None, :]).astype(
        jnp.bfloat16
    )
    chosen = jnp.dot(
        picker, recoup.reshape(recoup.shape[0], -1), preferred_element_type=jnp.float32
    )
    chosen = chosen.astype(jnp.bfloat16).reshape(-1, tile_size, tile_size)

    def recouple(matrix):
        return jnp.einsum(
            "kab,kbd->kad",
            split_tiles(matrix, tile_size),
            chosen,
            preferred_element_type=jnp.float32,
        ).astype(jnp.bfloat16)

    send_flat = send_slot.reshape(-1)
    recv_flat = recv_slot.reshape(-1)
    send_sorter = jnp.argsort(send_flat)
    eta_out = recouple(eta_local)[send_sorter]
    gamma_out = recouple(gamma_pair)[send_sorter]
    eta_in, gamma_in = (
        lax.all_to_all(eta_out, "chan", split_axis=0, concat_axis=0, tiled=True),
        lax.all_to_all(gamma_out, "chan", split_axis=0, concat_axis=0, tiled=True),
    )
    eta_cross = join_tiles(eta_in[recv_flat], row_count, full_width)
    gamma_cross = join_tiles(gamma_in[recv_flat], row_count, full_width)
    columns = eta_cross
    cross_half = jnp.einsum(
        "crk,ckn->crn",
        columns,
        lax.all_gather(gamma_cross, "tile", axis=1, tiled=True),
        preferred_element_type=jnp.float32,
    )
    cross_turned = jnp.swapaxes(
        lax.all_to_all(cross_half, "tile", split_axis=2, concat_axis=1, tiled=True), 1, 2
    )
    cross_sym = (cross_half - cross_turned).astype(jnp.bfloat16)
    recv_sorter = jnp.argsort(recv_flat)
    returned = lax.all_to_all(
        split_tiles(cross_sym, tile_size)[recv_sorter],
        "chan",
        split_axis=0,
        concat_axis=0,
        tiled=True,
    )
    pair_tiles = returned[send_flat]
    back_tiles = jnp.einsum("kab,kdb->kad", pair_tiles, chosen, preferred_element_type=jnp.float32)
    back_full = join_tiles(back_tiles, row_count, full_width)
    step_size = 1.0 / math.sqrt(full_width)
    return gamma_pair.astype(jnp.float32) + step_size * (ladder + back_full)


def solution(mesh):
    placed = (
        P("chan", "tile", None),
        P("chan", None),
        P("chan", None),
        P(),
        P("chan", "tile", None),
        P("chan", "tile", None),
        P("chan", "tile", None),
    )
    return jax.shard_map(
        on_device, mesh=mesh, in_specs=placed, out_specs=P("chan", "tile", None), check_vma=False
    )
```

profile of v0, /device:TPU:1, one launch (start us, length us, event | category | flops | bytes accessed | tf_op | source)
XLA Modules:
  0.0 425.3 jit_solution(1922815006967149226)
XLA Ops:
  25.2 13.2 %all-to-all-start.1 = ((bf16[64,128,128]{1,2,0:T(8,128)(2,1)}), bf16[64,128,128]{1,2,0:T(8,128)(2,1)}, u32[]{:S(2)}, u32[]{:S(2)}) async-start(bf16[64,128,128]{1,2,0:T(8,128)(2,1)} %gather_fusion.2), calls=%async_computation.1 | async-start | bytes 4194304 | tf_op jit(solution)/shard_map/all_to_all | solution.py:78
  38.6 49.5 %all-to-all-done.1 = bf16[64,128,128]{1,2,0:T(8,128)(2,1)} async-done(((bf16[64,128,128]{1,2,0:T(8,128)(2,1)}), bf16[64,128,128]{1,2,0:T(8,128)(2,1)}, u32[]{:S(2)}, u32[]{:S(2)}) %all-to-all-start.1) | async-done | bytes 2097184 | tf_op jit(solution)/shard_map/all_to_all | solution.py:78
  91.7 4.5 %copy.25 = bf16[4,16,128,128]{3,1,2,0:T(8,128)(2,1)} copy(bf16[4,16,128,128]{2,3,1,0:T(8,128)(2,1)} %bitcast.121) | data formatting | bytes 4194304 | tf_op jit(solution)/shard_map/reshape | solution.py:18
  96.2 4.2 reshape.386
  101.3 4.2 fusion.7
  105.5 5.6 %fusion.16 = bf16[4,16,128,128]{3,1,2,0:T(8,128)(2,1)S(1)} fusion(f32[16,128]{1,0:T(8,128)S(1)} %bitcast.128, f32[4,128]{1,0:T(4,128)S(1)} %bitcast.131, pred[16,128]{1,0:T(8,128)(4,1)S(1)} %bitcast.134, pred[4,128]{1,0:T(4,128)(4,1)S(1)} %bitcast.136, pred[16,128]{1,0:T(8,128)(4,1)S(1)} %bitcast.133, pred[4,128]{1,0:T(4,128)(4,1)S(1)} %bitcast.135, ...), kind=kLoop, calls=%fused_computation.25 | loop fusion | flops 10485760 | bytes 4209664 | tf_op jit(solution)/shard_map/transpose | solution.py:13
  113.7 3.9 gather_fusion
  117.6 7.3 %all-to-all-start = ((bf16[64,128,128]{2,1,0:T(8,128)(2,1)}), bf16[64,128,128]{2,1,0:T(8,128)(2,1)}, u32[]{:S(2)}, u32[]{:S(2)}) async-start(bf16[64,128,128]{2,1,0:T(8,128)(2,1)} %gather_fusion), calls=%async_computation | async-start | bytes 4194304 | tf_op jit(solution)/shard_map/all_to_all | solution.py:77
  125.6 48.9 %all-to-all-done = bf16[64,128,128]{2,1,0:T(8,128)(2,1)} async-done(((bf16[64,128,128]{2,1,0:T(8,128)(2,1)}), bf16[64,128,128]{2,1,0:T(8,128)(2,1)}, u32[]{:S(2)}, u32[]{:S(2)}) %all-to-all-start) | async-done | bytes 2097184 | tf_op jit(solution)/shard_map/all_to_all | solution.py:77
  178.2 4.3 %copy.22 = bf16[4,16,128,128]{3,1,2,0:T(8,128)(2,1)} copy(bf16[4,16,128,128]{3,2,1,0:T(8,128)(2,1)} %bitcast.119) | data formatting | bytes 4194304 | tf_op jit(solution)/shard_map/reshape | solution.py:18
  183.9 10.5 %fusion.11 = f32[1,512,2048]{2,1,0:T(8,128)} fusion(bf16[1,2048,2048]{2,1,0:T(8,128)(2,1)} %all-gather.8.cloned.1.call-done, bf16[64,8,16,128]{3,2,1,0:T(8,128)(2,1)} %bitcast.125), kind=kOutput, calls=%fused_computation.24 | convolution fusion | flops 4294967296 | bytes 14680064 | tf_op jit(solution)/shard_map/crk,ckn->crn/dot_general | solution.py:83
  194.4 11.2 %copy.26 = f32[1,512,2048]{1,0,2:T(1,128)} copy(f32[1,512,2048]{2,1,0:T(8,128)} %fusion.11) | data formatting | bytes 8388608 | tf_op jit(solution)/shard_map/crk,ckn->crn/dot_general | solution.py:83
  205.6 4.9 %all-to-all-start.2 = ((f32[1,512,2048]{1,0,2:T(1,128)}), f32[1,512,2048]{1,0,2:T(1,128)}, u32[]{:S(2)}, u32[]{:S(2)}) async-start(f32[1,512,2048]{1,0,2:T(1,128)} %copy.26), calls=%async_computation.2 | async-start | bytes 8388608 | tf_op jit(solution)/shard_map/all_to_all | solution.py:90
  210.5 94.1 %all-to-all-done.2 = f32[1,512,2048]{1,0,2:T(1,128)} async-done(((f32[1,512,2048]{1,0,2:T(1,128)}), f32[1,512,2048]{1,0,2:T(1,128)}, u32[]{:S(2)}, u32[]{:S(2)}) %all-to-all-start.2) | async-done | bytes 4194336 | tf_op jit(solution)/shard_map/all_to_all | solution.py:90
  304.5 6.9 %copy.47 = f32[1,512,4,512]{1,2,3,0:T(4,128)} copy(f32[1,512,4,512]{1,0,3,2:T(1,128)} %bitcast.20) | data formatting | bytes 8388608 | tf_op jit(solution)/shard_map/all_to_all | solution.py:90
  311.4 6.1 %all_to_all.27 = f32[1,2048,512]{1,2,0:T(8,128)} reshape(f32[1,4,512,512]{2,1,3,0:T(4,128)} %bitcast.116) | data formatting | bytes 8388608 | tf_op jit(solution)/shard_map/all_to_all | solution.py:90
  317.4 4.4 %fusion.17 = bf16[64,8,16,128]{3,1,2,0:T(8,128)(2,1)S(1)} fusion(f32[1,512,2048]{2,1,0:T(8,128)} %fusion.11, f32[1,2048,512]{1,2,0:T(8,128)} %all_to_all.27), kind=kLoop, calls=%fused_computation.26 | loop fusion | flops 2097152 | bytes 10485760
  328.0 11.7 %all-to-all-start.3 = ((bf16[64,128,128]{2,1,0:T(8,128)(2,1)}), bf16[64,128,128]{2,1,0:T(8,128)(2,1)}, u32[]{:S(2)}, u32[]{:S(2)}) async-start(bf16[64,128,128]{2,1,0:T(8,128)(2,1)} %gather_fusion.4), calls=%async_computation.3 | async-start | bytes 4194304 | tf_op jit(solution)/shard_map/all_to_all | solution.py:94
  339.9 10.6 %fusion.2 = f32[512,2048]{1,0:T(8,128)} fusion(bf16[1,2048,2048]{2,1,0:T(8,128)(2,1)} %all-gather.6.cloned.1.call-done, bf16[1,512,2048]{2,1,0:T(8,128)(2,1)} %param.7, bf16[2048]{0:T(1024)(128)(2,1)S(1)} %convert_reduce_fusion), kind=kOutput, calls=%fused_computation.9 | convolution fusion | flops 4296015872 | bytes 14684160 | tf_op jit(solution)/shard_map/crk,cnk->crn/dot_general | solution.py:47
  350.5 38.9 %all-to-all-done.3 = bf16[64,128,128]{2,1,0:T(8,128)(2,1)} async-done(((bf16[64,128,128]{2,1,0:T(8,128)(2,1)}), bf16[64,128,128]{2,1,0:T(8,128)(2,1)}, u32[]{:S(2)}, u32[]{:S(2)}) %all-to-all-start.3) | async-done | bytes 2097184 | tf_op jit(solution)/shard_map/all_to_all | solution.py:94
  389.4 3.8 gather_fusion.5
  396.3 4.4 %copy.29 = f32[4,16,128,128]{3,1,2,0:T(8,128)} copy(f32[4,16,128,128]{3,2,1,0:T(8,128)S(1)} %bitcast.115) | data formatting | bytes 8388608 | tf_op jit(solution)/shard_map/reshape | solution.py:18
  400.7 5.1 %all-gather.4.cloned.1.call-done = bf16[1,2048,2048]{2,1,0:T(8,128)(2,1)} async-done(((bf16[1,512,2048]{2,1,0:T(8,128)(2,1)}), bf16[1,2048,2048]{2,1,0:T(8,128)(2,1)}) %all-gather.4.cloned.1.call-update) | async-done | bytes 8388624 | tf_op jit(solution)/shard_map/all_gather | solution.py:43
  405.8 13.0 %convert_add_fusion = f32[1,512,2048]{2,1,0:T(8,128)} fusion(bf16[1,512,2048]{2,1,0:T(8,128)(2,1)S(1)} %copy-done, f32[64,8,16,128]{3,2,1,0:T(8,128)} %bitcast.124, f32[512,2048]{1,0:T(8,128)} %fusion.2, bf16[1,2048,2048]{2,1,0:T(8,128)(2,1)} %all-gather.4.cloned.1.call-done, bf16[2048]{0:T(1024)(128)(2,1)S(1)} %convert_reduce_fusion, ...), kind=kOutput, calls=%fused_computation.13 | convolution fusion | flops 4314890240 | bytes 23088128 | tf_op jit(solution)/shard_map/crk,ckn->crn/dot_general | solution.py:40
  (58 shorter events, 41.2 us)
Async XLA Ops:
  6.5 3.6 copy-start.6
  6.5 3.7 copy-start.1
  11.0 0.7 copy-start.5
  11.0 0.8 copy-start.4
  25.2 62.8 %all-to-all-start.1 = ((bf16[64,128,128]{1,2,0:T(8,128)(2,1)}), bf16[64,128,128]{1,2,0:T(8,128)(2,1)}, u32[]{:S(2)}, u32[]{:S(2)}) async-start(bf16[64,128,128]{1,2,0:T(8,128)(2,1)} %gather_fusion.2), calls=%async_computation.1 | async-start | bytes 4194304 | tf_op jit(solution)/shard_map/all_to_all | solution.py:78
  38.4 145.5 %all-gather.8.cloned.1.call-start = ((), (), s32[]{:S(2)}) async-start(), calls=%async_computation.6 | async-start | bytes 10485760 | tf_op jit(solution)/shard_map/all_gather | solution.py:86
  100.4 0.7 copy-start.2
  100.5 0.7 copy-start.3
  100.5 239.4 %all-gather.6.cloned.1.call-start = ((), (), s32[]{:S(2)}) async-start(), calls=%async_computation.5 | async-start | bytes 10485760 | tf_op jit(solution)/shard_map/all_gather | solution.py:50
  117.6 56.9 %all-to-all-start = ((bf16[64,128,128]{2,1,0:T(8,128)(2,1)}), bf16[64,128,128]{2,1,0:T(8,128)(2,1)}, u32[]{:S(2)}, u32[]{:S(2)}) async-start(bf16[64,128,128]{2,1,0:T(8,128)(2,1)} %gather_fusion), calls=%async_computation | async-start | bytes 4194304 | tf_op jit(solution)/shard_map/all_to_all | solution.py:77
  124.8 280.9 %all-gather.4.cloned.1.call-start = ((), (), s32[]{:S(2)}) async-start(), calls=%async_computation.4 | async-start | bytes 10485760 | tf_op jit(solution)/shard_map/all_gather | solution.py:43
  205.6 99.0 %all-to-all-start.2 = ((f32[1,512,2048]{1,0,2:T(1,128)}), f32[1,512,2048]{1,0,2:T(1,128)}, u32[]{:S(2)}, u32[]{:S(2)}) async-start(f32[1,512,2048]{1,0,2:T(1,128)} %copy.26), calls=%async_computation.2 | async-start | bytes 8388608 | tf_op jit(solution)/shard_map/all_to_all | solution.py:90
  328.0 61.4 %all-to-all-start.3 = ((bf16[64,128,128]{2,1,0:T(8,128)(2,1)}), bf16[64,128,128]{2,1,0:T(8,128)(2,1)}, u32[]{:S(2)}, u32[]{:S(2)}) async-start(bf16[64,128,128]{2,1,0:T(8,128)(2,1)} %gather_fusion.4), calls=%async_computation.3 | async-start | bytes 4194304 | tf_op jit(solution)/shard_map/all_to_all | solution.py:94
  396.3 9.5 %copy-start = (bf16[1,512,2048]{2,1,0:T(8,128)(2,1)S(1)}, bf16[1,512,2048]{2,1,0:T(8,128)(2,1)}, u32[]{:S(2)}) copy-start(bf16[1,512,2048]{2,1,0:T(8,128)(2,1)} %param.7) | copy-start | bytes 6291460
Sparse Core Ops, SparseCore 0:
  100.6 83.2 all-gather.7
  185.7 131.5 all-gather.5
  319.1 86.6 all-gather.3
where the time goes:
time: 427 us; the launch traced here: 425 us
  waiting for transfers between devices  238 us (56%)
  local copies, waits for them, and re-layouts  74.8 us (18%)
  matrix products  43 us (10%)
  starting transfers between devices  37.3 us (9%)
  other arithmetic  18.6 us (4%)
  between operations  13.3 us (3%)
    all_to_all x1, waiting for transfers between devices, on_device(): lax.all_to_all(cross_half, 'tile', split_axis=2, concat_axis=1, tiled=True)  94.1 us
    all_to_all x1, waiting for transfers between devices, on_device(): lax.all_to_all(gamma_out, 'chan', split_axis=0, concat_axis=0, tiled=True)  49.5 us
    all_to_all x1, waiting for transfers between devices, on_device(): lax.all_to_all(eta_out, 'chan', split_axis=0, concat_axis=0, tiled=True)  48.9 us
    all_to_all x1, waiting for transfers between devices, on_device(): lax.all_to_all(split_tiles(cross_sym, tile_size)[recv_sorter], 'chan', sp...  38.9 us
    reshape x3, local copies, waits for them, and re-layouts, join_tiles(): tile_set.reshape(row_count // tile_size, full_width // tile_size, tile_si...  13.2 us
    all_to_all x1, starting transfers between devices, on_device(): lax.all_to_all(gamma_out, 'chan', split_axis=0, concat_axis=0, tiled=True)  13.2 us
    dot_general x1, matrix products, on_device(): jnp.einsum('crk,ckn->crn', columns, lax.all_gather(gamma_pair, 'tile', ax...  13 us
    all_to_all x2, local copies, waits for them, and re-layouts, on_device(): lax.all_to_all(cross_half, 'tile', split_axis=2, concat_axis=1, tiled=True)  12.9 us
  transfers between devices with their start and end apart: 7, of which 6 were waited for; matrix products, arithmetic and copies ran while one was open for 20% of the time, Pallas kernels for 0%

commit v1 on v0

v1 whole, which is shorter than its diff:
```python
import functools
import math

import jax
import jax.numpy as jnp
from jax import lax
from jax.experimental import pallas as pl
from jax.experimental.pallas import tpu as pltpu
from jax.sharding import PartitionSpec as P


BF = jnp.bfloat16
F32 = jnp.float32
TB = 128
META = 8
CHUNKS = 2
ROWS = TB // CHUNKS
SMEM = pl.BlockSpec(memory_space=pltpu.SMEM)
VMEM = pl.BlockSpec(memory_space=pltpu.VMEM)
ANY = pl.BlockSpec(memory_space=pl.ANY)
BIG = pltpu.CompilerParams(vmem_limit_bytes=60 << 20)


def coded(energy, occ):
    return jnp.where(occ == 0, energy, jnp.where(occ == 2, -energy, 0.0))


def pack_kernel(chunk, tiles_across, me, send, cls, gamma, energy, occ, buf, row_pieces, col_pieces):
    if chunk == 0:
        value = coded(energy[...], occ[...])
        first = value.astype(BF).astype(F32)
        rest = value - first
        second = rest.astype(BF).astype(F32)
        third = rest - second
        row_pieces[...] = jnp.zeros_like(row_pieces)
        col_pieces[...] = jnp.zeros_like(col_pieces)
        for n, piece in enumerate((first, second, third)):
            row_pieces[n : n + 1, :] = piece
            col_pieces[n + 3 : n + 4, :] = piece
    rows_down = gamma.shape[0] // TB

    def body(k, carry):
        i, j = k // tiles_across, k % tiles_across
        across = pl.ds(pl.multiple_of(j * TB, TB), TB)
        slot = send[i, j]
        buf[slot, 0:ROWS, :] = gamma[pl.ds(pl.multiple_of(i * TB + chunk * ROWS, ROWS), ROWS), across]
        if chunk == 0:
            down = pl.ds(pl.multiple_of((me[0] * rows_down + i) * TB, TB), TB)
            line = lax.broadcasted_iota(jnp.int32, (META, TB), 0)
            head = row_pieces[:, down] + col_pieces[:, across]
            head = head + jnp.where(line == 6, cls[i, j].astype(F32), 0.0)
            buf[slot, ROWS : ROWS + META, :] = head.astype(BF)
        return carry

    lax.fori_loop(0, rows_down * tiles_across, body, 0, unroll=8)


def pack(chunk, me, send, cls, gamma, energy, occ):
    rows = ROWS + (META if chunk == 0 else 0)
    return pl.pallas_call(
        functools.partial(pack_kernel, chunk, gamma.shape[1] // TB),
        out_shape=jax.ShapeDtypeStruct((send.size, rows, TB), BF),
        in_specs=[SMEM] * 3 + [VMEM] * 3,
        out_specs=VMEM,
        scratch_shapes=[pltpu.VMEM((META, gamma.shape[1]), F32)] * 2,
    )(me, send, cls, gamma, energy, occ)


def tables_kernel(own, right, far, left, out):
    for n, table in enumerate((own, right, far, left)):
        out[n] = table[...]


def join_tables(*tables):
    return pl.pallas_call(
        tables_kernel,
        out_shape=jax.ShapeDtypeStruct((4,) + tables[0].shape, jnp.int32),
        in_specs=[VMEM] * 4,
        out_specs=VMEM,
        name="join_tables",
    )(*tables)


def share_kernel(me, gamma, right, left):
    side = gamma.shape[0]
    half = side // 2

    def block(offset):
        return pl.ds(pl.multiple_of(((me[0] + offset) % 4) * side, side), side)

    own = gamma[:, block(0)]
    right[0:side, :] = own
    left[0:side, :] = own
    right[side : 2 * side, :] = gamma[:, block(3)]
    left[side : 2 * side, :] = gamma[:, block(1)]
    far = gamma[:, block(2)]
    right[2 * side :, :] = far[0:half]
    left[2 * side :, 0:half] = far[0:half, half:]
    left[2 * side :, half:] = far[half:, half:]


def share(me, gamma):
    side = gamma.shape[0]
    shape = jax.ShapeDtypeStruct((2 * side + side // 2, side), BF)
    return pl.pallas_call(
        share_kernel,
        out_shape=[shape, shape],
        in_specs=[SMEM, VMEM],
        out_specs=[VMEM, VMEM],
        name="share_blocks",
    )(me, gamma)


def ladder_kernel(step_size, me, gamma, from_left, from_right, far_a, far_b, energy, occ, base, full, scaled, column):
    side = gamma.shape[0]
    half = side // 2
    width = gamma.shape[1]

    def put(a, b, value, row=0, col=0):
        rows = pl.ds(pl.multiple_of(((me[0] + a) % 4) * side + row, half), value.shape[0])
        cols = pl.ds(pl.multiple_of(((me[0] + b) % 4) * side + col, half), value.shape[1])
        full[rows, cols] = value

    def turn(value):
        return jnp.transpose(value.astype(F32)).astype(BF)

    mine = pl.ds(pl.multiple_of(me[0] * side, side), side)
    full[mine, :] = gamma[...]
    for b in range(1, 4):
        cols = pl.ds(pl.multiple_of(((me[0] + b) % 4) * side, side), side)
        put(b, 0, turn(gamma[:, cols]))
    put(3, 3, from_left[0:side, :])
    put(3, 2, from_left[side : 2 * side, :])
    put(2, 3, turn(from_left[side : 2 * side, :]))
    put(3, 1, from_left[2 * side :, :])
    put(1, 3, turn(from_left[2 * side :, :]))
    put(1, 1, from_right[0:side, :])
    put(1, 2, from_right[side : 2 * side, :])
    put(2, 1, turn(from_right[side : 2 * side, :]))
    for n in range(2):
        piece = from_right[2 * side :, n * half : (n + 1) * half]
        put(1, 3, piece, row=n * half, col=half)
        put(3, 1, turn(piece), row=half, col=n * half)
    put(2, 2, far_a[...])
    put(2, 2, far_b[...], row=half)

    value = coded(energy[...], occ[...])
    column[...] = jnp.transpose(jnp.broadcast_to(value, (8, width)))

    def scale(n, carry):
        rows = pl.ds(pl.multiple_of(n * 64, 64), 64)
        down = column[rows, 0:1]
        ratio = -full[rows, :].astype(F32) / jnp.abs(down - value)
        scaled[rows, :] = jnp.where(down * value < 0.0, ratio, 0.0).astype(BF)
        return carry

    lax.fori_loop(0, width // 64, scale, 0)

    def product(n, carry):
        cols = pl.ds(pl.multiple_of(n * 256, 256), 256)
        total = jnp.dot(scaled[mine, :], full[:, cols], preferred_element_type=F32)
        total = total + jnp.dot(full[mine, :], scaled[:, cols], preferred_element_type=F32)
        base[:, cols] = gamma[:, cols].astype(F32) + step_size * total
        return carry

    lax.fori_loop(0, width // 256, product, 0)


def ladder_base(step_size, me, gamma, from_left, from_right, far_a, far_b, energy, occ):
    width = gamma.shape[1]
    return pl.pallas_call(
        functools.partial(ladder_kernel, step_size),
        out_shape=jax.ShapeDtypeStruct(gamma.shape, F32),
        in_specs=[SMEM] + [VMEM] * 7,
        out_specs=VMEM,
        scratch_shapes=[
            pltpu.VMEM((width, width), BF),
            pltpu.VMEM((width, width), BF),
            pltpu.VMEM((width, 8), F32),
        ],
        compiler_params=BIG,
        name="ladder",
    )(me, gamma, from_left, from_right, far_a, far_b, energy, occ)


def decode(head, picks, down, along, cls, cls_int, sem):
    count = down.shape[1]
    lines = jnp.dot(picks[...], head, preferred_element_type=F32)
    side = jnp.concatenate([lines[0:count], jnp.zeros((TB - count, TB), F32)], axis=0) if count < TB else lines[0:count]
    down[...] = jnp.transpose(side)[:, 0:count]
    along[...] = lines[count : 2 * count]
    cls_int[...] = lines[2 * count :].astype(jnp.int32)
    copy = pltpu.make_async_copy(cls_int, cls, sem)
    copy.start()
    copy.wait()


def fill_picks(picks, count):
    row = lax.broadcasted_iota(jnp.int32, picks.shape, 0)
    col = lax.broadcasted_iota(jnp.int32, picks.shape, 1)
    kind, line = row // count, col % META
    hit = ((kind == 2) & (line == 6)) | ((kind < 2) & (line >= 3 * kind) & (line < 3 * kind + 3))
    picks[...] = jnp.where((col // META == row % count) & hit, 1.0, 0.0).astype(BF)


def recouple_block(chunk, across, raw, block, recv, recoup, scratch, put):
    down, along, cls, eta = scratch
    count = raw.shape[0]
    for q in range(count):
        column = down[chunk * ROWS : (chunk + 1) * ROWS, q : q + 1]
        line = along[q : q + 1, :]
        ratio = raw[q].astype(F32) / (column - line)
        eta[q] = jnp.where(column * line < 0.0, ratio, 0.0).astype(BF)

    def body(p, carry):
        i, j = p // across, p % across
        q = recv[block, i, j]
        both = jnp.concatenate([eta[q], raw[q]], axis=0)
        done = jnp.dot(both, recoup[cls[q, 0]], preferred_element_type=F32).astype(BF)
        put(i, pl.ds(pl.multiple_of(j * TB, TB), TB), done[0:ROWS], done[ROWS:])
        return carry

    lax.fori_loop(0, count, body, 0, unroll=8)


def block_scratch(groups, count):
    return [
        pltpu.VMEM((groups, count, ROWS, TB), BF),
        pltpu.VMEM((groups, count, META, TB), BF),
        pltpu.VMEM((3 * count, count * META), BF),
        pltpu.VMEM((TB, count), F32),
        pltpu.VMEM((count, TB), F32),
        pltpu.VMEM((count, TB), jnp.int32),
        pltpu.SMEM((count, TB), jnp.int32),
        pltpu.VMEM((count, ROWS, TB), BF),
        pltpu.SemaphoreType.DMA((groups, 5)),
    ]


def waits(raws, heads, raw, head, sems):
    copies, start = [], 0
    for n, (source, top) in enumerate(zip(raws, heads)):
        where = pl.ds(start, source.shape[0])
        start += source.shape[0]
        copies.append(pltpu.make_async_copy(top.at[:, ROWS : ROWS + META, :], head.at[where], sems.at[2 * n + 1]))
        copies.append(pltpu.make_async_copy(source.at[:, 0:ROWS, :], raw.at[where], sems.at[2 * n]))
    return copies


def fetch(*refs):
    copies = waits(*refs)
    for copy in copies:
        copy.start()
    return copies


def recouple_kernel(chunk, across, parts, blocks, recv, recoup, *refs):
    total = parts * len(blocks)
    raws, heads, refs = refs[:total], refs[total : 2 * total], refs[2 * total :]
    eta_out, gamma_out, raw, head, picks, down, along, cls_int, cls, eta, sems = refs
    for n in range(len(blocks)):
        span = slice(n * parts, (n + 1) * parts)
        fetch(raws[span], heads[span], raw.at[n], head.at[n], sems.at[n])
    count = raw.shape[1]
    high = eta_out.shape[0] // len(blocks)
    fill_picks(picks, count)

    def group(n, carry):
        block = sum(jnp.where(n == k, b, 0) for k, b in enumerate(blocks))
        for copy in waits(raws[:parts], heads[:parts], raw.at[n], head.at[n], sems.at[n]):
            copy.wait()
        decode(head[n].reshape(count * META, TB), picks, down, along, cls, cls_int, sems.at[n, 4])

        def put(i, cols, eta_tile, gamma_tile):
            eta_out[n * high + i, :, cols] = eta_tile
            gamma_out[n * high + i, :, cols] = gamma_tile

        recouple_block(chunk, across, raw.at[n], block, recv, recoup, (down, along, cls, eta), put)
        return carry

    lax.fori_loop(0, len(blocks), group, 0)


def recouple(chunk, across, blocks, tables, recoup, raws, heads):
    parts = len(raws[0])
    count = sum(raw.shape[0] for raw in raws[0])
    shape = jax.ShapeDtypeStruct((len(blocks) * count // across, ROWS, across * TB), BF)
    return pl.pallas_call(
        functools.partial(recouple_kernel, chunk, across, parts, blocks),
        out_shape=[shape, shape],
        in_specs=[SMEM, VMEM] + [ANY] * (2 * parts * len(blocks)),
        out_specs=[VMEM, VMEM],
        scratch_shapes=block_scratch(len(blocks), count),
        compiler_params=BIG,
    )(tables, recoup, *[r for group in raws for r in group], *[r for group in heads for r in group])


def cross_kernel(chunk, blocks, parts, me, recv, recoup, *refs):
    groups = len(set(key for _, _, key, _ in blocks))
    pieces, refs = refs[: 2 * groups], refs[2 * groups :]
    raws, heads, refs = refs[:parts], refs[parts : 2 * parts], refs[2 * parts :]
    out, eta, gamma, turned, piece_sems = refs[:5]
    raw, head, picks, down, along, cls_int, cls, eta_raw, sems = refs[5:]
    rows_down = recv.shape[1]
    width = pieces[0].shape[2]
    late = fetch(raws, heads, raw.at[0], head.at[0], sems.at[0])
    copies = []
    for n, (part, block, key, place) in enumerate(blocks):
        where = pl.ds(((me[0] + block) % 4) * rows_down, rows_down)
        for which, target in enumerate((eta, gamma)):
            source = pieces[2 * key + which].at[pl.ds(place * rows_down, rows_down)]
            into = target.at[where, pl.ds(part * ROWS, ROWS), :]
            copies.append(pltpu.make_async_copy(source, into, piece_sems.at[2 * n + which]))
    for copy in copies:
        copy.start()
    count = raw.shape[1]
    fill_picks(picks, count)
    for copy in late:
        copy.wait()
    decode(head[0].reshape(count * META, TB), picks, down, along, cls, cls_int, sems.at[0, 4])
    far = ((me[0] + 2) % 4) * rows_down

    def put(i, cols, eta_tile, gamma_tile):
        eta[far + i, chunk * ROWS : (chunk + 1) * ROWS, cols] = eta_tile
        gamma[far + i, chunk * ROWS : (chunk + 1) * ROWS, cols] = gamma_tile

    recouple_block(chunk, width // TB, raw.at[0], 2, recv, recoup, (down, along, cls, eta_raw), put)
    for copy in copies:
        copy.wait()
    side = rows_down * TB
    mine = pl.ds(me[0] * rows_down, rows_down)
    for i in range(rows_down):
        cols = pl.ds(pl.multiple_of((me[0] * rows_down + i) * TB, TB), TB)
        for k in range(4 * rows_down):
            tile = gamma[k, :, cols].astype(F32)
            turned[i * TB : (i + 1) * TB, k * TB : (k + 1) * TB] = jnp.transpose(tile).astype(BF)
    step = 2

    def body(n, carry):
        cols = pl.ds(pl.multiple_of(n * step * TB, step * TB), step * TB)
        half = jnp.dot(
            eta[mine].reshape(side, width),
            gamma[:, :, cols].reshape(width, step * TB),
            preferred_element_type=F32,
        )
        other = lax.dot_general(
            turned[...],
            eta[pl.ds(n * step, step)].reshape(step * TB, width),
            (((1,), (1,)), ((), ())),
            preferred_element_type=F32,
        )
        result = (half - other).astype(BF)
        for i in range(rows_down):
            for j in range(step):
                out[recv[0, i, n * step + j]] = result[i * TB : (i + 1) * TB, j * TB : (j + 1) * TB]
        return carry

    lax.fori_loop(0, width // (step * TB), body, 0)


def cross(chunk, me, tables, recoup, pieces, raws, heads):
    flat = [array for _, _, pair in pieces for array in pair]
    blocks = tuple(
        (part, block, key, place)
        for key, (part, members, _) in enumerate(pieces)
        for place, block in enumerate(members)
    )
    rows_down, width = tables.shape[1], flat[0].shape[2]
    return pl.pallas_call(
        functools.partial(cross_kernel, chunk, blocks, len(raws)),
        out_shape=jax.ShapeDtypeStruct((tables[0].size, TB, TB), BF),
        in_specs=[SMEM] * 2 + [VMEM] + [ANY] * (len(flat) + 2 * len(raws)),
        out_specs=VMEM,
        scratch_shapes=[
            pltpu.VMEM((4 * rows_down, TB, width), BF),
            pltpu.VMEM((4 * rows_down, TB, width), BF),
            pltpu.VMEM((rows_down * TB, width), BF),
            pltpu.SemaphoreType.DMA((2 * len(blocks),)),
        ]
        + block_scratch(1, tables[0].size),
        compiler_params=BIG,
        name="cross",
    )(me, tables, recoup, *flat, *raws, *heads)


def final_kernel(step_size, send, cls, base, back, recoup, out):
    i = pl.program_id(0)
    for j in range(base.shape[1] // TB):
        cols = slice(j * TB, (j + 1) * TB)
        turned = lax.dot_general(
            back[send[i, j]], recoup[cls[i, j]], (((1,), (1,)), ((), ())), preferred_element_type=F32
        )
        out[:, cols] = base[:, cols] + step_size * turned


def finish(step_size, send, cls, base, back, recoup):
    width = base.shape[1]
    rows = pl.BlockSpec((TB, width), lambda i: (i, 0))
    return pl.pallas_call(
        functools.partial(final_kernel, step_size),
        grid=(base.shape[0] // TB,),
        out_shape=jax.ShapeDtypeStruct(base.shape, F32),
        in_specs=[
            SMEM,
            SMEM,
            rows,
            pl.BlockSpec(back.shape, lambda i: (0, 0, 0)),
            pl.BlockSpec(recoup.shape, lambda i: (0, 0, 0)),
        ],
        out_specs=rows,
        name="finish",
    )(send, cls, base, back, recoup)


RIGHT = [(i, (i + 1) % 4) for i in range(4)]
LEFT = [(i, (i + 3) % 4) for i in range(4)]
ACROSS = [(i, (i + 2) % 4) for i in range(4)]


def on_device(gamma_pair, energies, occupancy, recoup, recoup_class, send_slot, recv_slot):
    gamma = gamma_pair[0]
    width = gamma.shape[1]
    across = width // TB
    step_size = 1.0 / math.sqrt(width)
    me = lax.axis_index("tile").astype(jnp.int32).reshape(1)
    send, recv, cls = send_slot[0], recv_slot[0], recoup_class[0]

    arrived = []
    for h in range(CHUNKS):
        buf = pack(h, me, send, cls, gamma, energies, occupancy)
        arrived.append(lax.all_to_all(buf, "chan", split_axis=0, concat_axis=0, tiled=True))
    to_right, to_left = share(me, gamma)
    half = gamma.shape[0] // 2
    from_left = lax.ppermute(to_right, "tile", RIGHT)
    from_right = lax.ppermute(to_left, "tile", LEFT)
    far_a = lax.ppermute(from_left[0:half], "tile", RIGHT)
    far_b = lax.ppermute(from_right[half : 2 * half], "tile", LEFT)
    tables = join_tables(
        recv,
        lax.ppermute(recv, "tile", LEFT),
        lax.ppermute(recv, "tile", ACROSS),
        lax.ppermute(recv, "tile", RIGHT),
    )
    base = ladder_base(step_size, me, gamma, from_left, from_right, far_a, far_b, energies, occupancy)

    pieces, heads = [], None

    def form(chunk, members, raws, tops):
        pieces.append((chunk, members, recouple(chunk, across, members, tables, recoup, raws, tops)))

    for h in range(CHUNKS):
        own = arrived[h]
        mid = own.shape[0] // 2
        left = lax.ppermute(own, "tile", RIGHT)
        right = lax.ppermute(own, "tile", LEFT)
        opposite = [lax.ppermute(left[0:mid], "tile", RIGHT), lax.ppermute(right[mid:], "tile", LEFT)]
        if h == 0:
            heads = ([own], [right], opposite, [left])
        if h + 1 < CHUNKS:
            form(h, (0, 1, 3), ([own], [right], [left]), (heads[0], heads[1], heads[3]))
            form(h, (2,), (opposite,), (heads[2],))
        else:
            form(h, (0,), ([own],), (heads[0],))
            form(h, (1, 3), ([right], [left]), (heads[1], heads[3]))
    crossed = cross(CHUNKS - 1, me, tables, recoup, pieces, opposite, heads[2])
    back = lax.all_to_all(crossed, "chan", split_axis=0, concat_axis=0, tiled=True)
    return finish(step_size, send, cls, base, back, recoup)[None]


def solution(mesh):
    placed = (
        P("chan", "tile", None),
        P("chan", None),
        P("chan", None),
        P(),
        P("chan", "tile", None),
        P("chan", "tile", None),
        P("chan", "tile", None),
    )
    return jax.shard_map(
        on_device, mesh=mesh, in_specs=placed, out_specs=P("chan", "tile", None), check_vma=False
    )
```

time: 427 us -> 299 us (0.70)
  waiting for transfers between devices: 238 us -> 127 us
  Pallas kernels: 0 us -> 110 us
  local copies, waits for them, and re-layouts: 74.8 us -> 8.88 us
  matrix products: 43 us -> 0 us
  other arithmetic: 18.6 us -> 0 us
  starting transfers between devices: 37.3 us -> 50.5 us
  between operations: 13.3 us -> 0.19 us
    all_to_all x4 -> x3, waiting for transfers between devices: 231 us -> 52.4 us  [the longest x2 52.4 us: on_device(): lax.all_to_all(buf, 'chan', split_axis=0, concat_axis=0, tiled=True)]
    pallas_call x0 -> x11, Pallas kernels: none -> 110 us  [the longest x4 44.3 us: recouple(): pl.pallas_call(functools.partial(recouple_kernel, chunk, across, parts, b...]
    ppermute x0 -> x15, waiting for transfers between devices: none -> 74.3 us  [the longest x1 28.6 us: on_device(): from_left = lax.ppermute(to_right, 'tile', RIGHT)]
    dot_general x7 -> x0, matrix products: 43 us -> none  [the longest x1 13 us: on_device(): jnp.einsum('crk,ckn->crn', columns, lax.all_gather(gamma_pair, 'tile', ax...]
    gather x6 -> x0, local copies, waits for them, and re-layouts: 22.5 us -> none  [the longest x1 3.87 us: on_device(): eta_out = recouple(eta_local)[send_sorter]]
    reshape x9 -> x0, local copies, waits for them, and re-layouts: 19.6 us -> none  [the longest x3 13.2 us: join_tiles(): tile_set.reshape(row_count // tile_size, full_width // tile_size, tile_si...]
    ppermute x0 -> x15, starting transfers between devices: none -> 19.5 us  [the longest x2 4.25 us: on_device(): right = lax.ppermute(own, 'tile', LEFT)]
    all_to_all x2 -> x0, local copies, waits for them, and re-layouts: 12.9 us -> none  [on_device(): lax.all_to_all(cross_half, 'tile', split_axis=2, concat_axis=1, tiled=True)]
  transfers between devices with their start and end apart: 7 -> 18, of which waited for: 6 -> 9; matrix products, arithmetic and copies ran while one was open for 20% -> 1% of each run, Pallas kernels for 0% -> 26%
where the time goes in v1:
time: 299 us; the launch traced here: 297 us
  waiting for transfers between devices  127 us (42%)
  Pallas kernels  110 us (37%)
  starting transfers between devices  50.5 us (17%)
  local copies, waits for them, and re-layouts  8.88 us (3%)
    all_to_all x2, waiting for transfers between devices, on_device(): lax.all_to_all(buf, 'chan', split_axis=0, concat_axis=0, tiled=True)  52.4 us
    pallas_call x4, Pallas kernels, recouple(): pl.pallas_call(functools.partial(recouple_kernel, chunk, across, parts, b...  44.3 us
    ppermute x1, waiting for transfers between devices, on_device(): from_left = lax.ppermute(to_right, 'tile', RIGHT)  28.6 us
    pallas_call x1, Pallas kernels, ladder_base(): pl.pallas_call(functools.partial(ladder_kernel, step_size), out_shape=jax...  25.5 us
    pallas_call x1, Pallas kernels, cross(): pl.pallas_call(functools.partial(cross_kernel, chunk, blocks, len(raws)),...  22.6 us
    all_to_all x2, starting transfers between devices, on_device(): lax.all_to_all(buf, 'chan', split_axis=0, concat_axis=0, tiled=True)  19.8 us
    ppermute x2, waiting for transfers between devices, on_device(): left = lax.ppermute(own, 'tile', RIGHT)  19 us
    ppermute x1, waiting for transfers between devices, on_device(): lax.ppermute(recv, 'tile', LEFT)  18.9 us
  transfers between devices with their start and end apart: 18, of which 9 were waited for; matrix products, arithmetic and copies ran while one was open for 1% of the time, Pallas kernels for 26%

profile of v1, /device:TPU:1, one launch (start us, length us, event | category | flops | bytes accessed | tf_op | source)
XLA Modules:
  0.0 296.7 jit_solution(2481535733393870945)
XLA Ops:
  0.0 3.7 %shard_map.73 = bf16[64,72,128]{2,1,0:T(8,128)(2,1)} custom-call(s32[1]{0:T(128)} %bitcast.2.me, s32[4,16]{1,0:T(4,128)} %bitcast.10, s32[4,16]{1,0:T(4,128)} %bitcast.13, bf16[512,2048]{1,0:T(8,128)(2,1)} %bitcast.6, f32[1,2048]{1,0:T(1,128)} %energy.5, s32[1,2048]{1,0:T(1,128)} %occ.5), custom_call_target="tpu_custom_call" | custom-call | tf_op jit(solution)/shard_map/pallas_call | solution.py:60
  3.7 13.0 %all-to-all-start = ((bf16[64,72,128]{2,1,0:T(8,128)(2,1)}), bf16[64,72,128]{2,1,0:T(8,128)(2,1)S(1)}, u32[]{:S(2)}, u32[]{:S(2)}) async-start(bf16[64,72,128]{2,1,0:T(8,128)(2,1)} %shard_map.73), calls=%async_computation | async-start | bytes 2359296 | tf_op jit(solution)/shard_map/all_to_all | solution.py:431
  16.7 3.5 %shard_map.76 = bf16[64,64,128]{2,1,0:T(8,128)(2,1)} custom-call(s32[1]{0:T(128)} %bitcast.2.me, s32[4,16]{1,0:T(4,128)} %bitcast.11, s32[4,16]{1,0:T(4,128)} %bitcast.14, bf16[512,2048]{1,0:T(8,128)(2,1)} %bitcast.7, f32[1,2048]{1,0:T(1,128)} %energy.5, s32[1,2048]{1,0:T(1,128)} %occ.5), custom_call_target="tpu_custom_call" | custom-call | tf_op jit(solution)/shard_map/pallas_call | solution.py:60
  20.1 27.1 %all-to-all-done.refs_0_.refs_3_.refs_1_ = bf16[64,72,128]{2,1,0:T(8,128)(2,1)S(1)} async-done(((bf16[64,72,128]{2,1,0:T(8,128)(2,1)}), bf16[64,72,128]{2,1,0:T(8,128)(2,1)S(1)}, u32[]{:S(2)}, u32[]{:S(2)}) %all-to-all-start) | async-done | bytes 1179680 | tf_op jit(solution)/shard_map/all_to_all | solution.py:431
  47.3 6.8 %all-to-all-start.1 = ((bf16[64,64,128]{2,1,0:T(8,128)(2,1)}), bf16[64,64,128]{2,1,0:T(8,128)(2,1)}, u32[]{:S(2)}, u32[]{:S(2)}) async-start(bf16[64,64,128]{2,1,0:T(8,128)(2,1)} %shard_map.76), calls=%async_computation.1 | async-start | bytes 2097152 | tf_op jit(solution)/shard_map/all_to_all | solution.py:431
  54.1 2.8 collective-permute-start.7
  56.9 25.3 %all-to-all-done.1.refs_0_ = bf16[64,64,128]{2,1,0:T(8,128)(2,1)} async-done(((bf16[64,64,128]{2,1,0:T(8,128)(2,1)}), bf16[64,64,128]{2,1,0:T(8,128)(2,1)}, u32[]{:S(2)}, u32[]{:S(2)}) %all-to-all-start.1) | async-done | bytes 1048608 | tf_op jit(solution)/shard_map/all_to_all | solution.py:431
  88.3 19.0 %collective-permute-done.12.refs_1_ = bf16[64,64,128]{2,1,0:T(8,128)(2,1)S(1)} collective-permute-done((bf16[64,64,128]{2,1,0:T(8,128)(2,1)}, bf16[64,64,128]{2,1,0:T(8,128)(2,1)S(1)}, u32[]{:S(2)}, u32[]{:S(2)}) %collective-permute-start.12) | collective-permute-done | bytes 1048608 | tf_op jit(solution)/shard_map/ppermute | solution.py:454
  109.1 2.7 collective-permute-start.14
  112.0 18.9 %collective-permute-done.4.right = s32[4,16]{1,0:T(4,128)S(1)} collective-permute-done((s32[4,16]{1,0:T(4,128)S(1)}, s32[4,16]{1,0:T(4,128)S(1)}, u32[]{:S(2)}, u32[]{:S(2)}) %collective-permute-start.4) | collective-permute-done | bytes 288 | tf_op jit(solution)/shard_map/ppermute | solution.py:440
  130.9 2.6 collective-permute-start.5
  140.4 7.6 %shard_map.77 = (bf16[4,64,2048]{2,1,0:T(8,128)(2,1)}, bf16[4,64,2048]{2,1,0:T(8,128)(2,1)}) custom-call(s32[4,4,16]{2,1,0:T(4,128)} %join_tables.1.recv, bf16[8,128,128]{2,1,0:T(8,128)(2,1)} %recoup.11, bf16[64,64,128]{2,1,0:T(8,128)(2,1)} %all-to-all-done.1.refs_0_, bf16[64,72,128]{2,1,0:T(8,128)(2,1)} %copy-done), custom_call_target="tpu_custom_call" | custom-call | tf_op jit(solution)/shard_map/pallas_call | solution.py:288
  148.0 12.3 %shard_map.78 = (bf16[8,64,2048]{2,1,0:T(8,128)(2,1)}, bf16[8,64,2048]{2,1,0:T(8,128)(2,1)}) custom-call(s32[4,4,16]{2,1,0:T(4,128)} %join_tables.1.recv, bf16[8,128,128]{2,1,0:T(8,128)(2,1)} %recoup.11, bf16[64,64,128]{2,1,0:T(8,128)(2,1)} %copy-done.5, bf16[64,64,128]{2,1,0:T(8,128)(2,1)} %copy-done.4, bf16[64,72,128]{2,1,0:T(8,128)(2,1)} %copy-done.1, ...), custom_call_target="tpu_custom_call" | custom-call | tf_op jit(solution)/shard_map/pallas_call | solution.py:288
  160.4 16.8 %shard_map.74 = (bf16[12,64,2048]{2,1,0:T(8,128)(2,1)}, bf16[12,64,2048]{2,1,0:T(8,128)(2,1)}) custom-call(s32[4,4,16]{2,1,0:T(4,128)} %join_tables.1.recv, bf16[8,128,128]{2,1,0:T(8,128)(2,1)} %recoup.11, bf16[64,72,128]{2,1,0:T(8,128)(2,1)} %copy-done, bf16[64,72,128]{2,1,0:T(8,128)(2,1)} %copy-done.1, bf16[64,72,128]{2,1,0:T(8,128)(2,1)} %copy-done.2, ...), custom_call_target="tpu_custom_call" | custom-call | tf_op jit(solution)/shard_map/pallas_call | solution.py:288
  177.2 7.5 %shard_map.75 = (bf16[4,64,2048]{2,1,0:T(8,128)(2,1)}, bf16[4,64,2048]{2,1,0:T(8,128)(2,1)}) custom-call(s32[4,4,16]{2,1,0:T(4,128)} %join_tables.1.recv, bf16[8,128,128]{2,1,0:T(8,128)(2,1)} %recoup.11, bf16[32,72,128]{2,1,0:T(8,128)(2,1)} %collective-permute-done.9.refs_0_.refs_2_.refs_10_, ...), custom_call_target="tpu_custom_call" | custom-call | tf_op jit(solution)/shard_map/pallas_call | solution.py:288
  185.8 22.6 %cross.1 = bf16[64,128,128]{2,1,0:T(8,128)(2,1)} custom-call(s32[1]{0:T(128)} %bitcast.2.me, s32[4,4,16]{2,1,0:T(4,128)} %join_tables.1.recv, bf16[8,128,128]{2,1,0:T(8,128)(2,1)} %recoup.11, bf16[12,64,2048]{2,1,0:T(8,128)(2,1)} %get-tuple-element.17.refs_0_, bf16[12,64,2048]{2,1,0:T(8,128)(2,1)} %get-tuple-element.18.refs_1_, ...), custom_call_target="tpu_custom_call" | custom-call | tf_op jit(solution)/shard_map/cross/pallas_call | solution.py:369
  208.4 11.2 %all-to-all-start.2 = ((bf16[64,128,128]{2,1,0:T(8,128)(2,1)}), bf16[64,128,128]{2,1,0:T(8,128)(2,1)S(1)}, u32[]{:S(2)}, u32[]{:S(2)}) async-start(bf16[64,128,128]{2,1,0:T(8,128)(2,1)} %cross.1), calls=%async_computation.2 | async-start | bytes 4194304 | tf_op jit(solution)/shard_map/all_to_all | solution.py:466
  219.6 3.3 %share_blocks.1 = (bf16[1280,512]{1,0:T(8,128)(2,1)}, bf16[1280,512]{1,0:T(8,128)(2,1)}) custom-call(s32[1]{0:T(128)} %bitcast.2.me, bf16[512,2048]{1,0:T(8,128)(2,1)} %bitcast.8), custom_call_target="tpu_custom_call" | custom-call | tf_op jit(solution)/shard_map/share_blocks/pallas_call | solution.py:105
  222.9 2.7 collective-permute-start.1
  225.6 28.6 %collective-permute-done.from_left = bf16[1280,512]{1,0:T(8,128)(2,1)S(1)} collective-permute-done((bf16[1280,512]{1,0:T(8,128)(2,1)}, bf16[1280,512]{1,0:T(8,128)(2,1)S(1)}, u32[]{:S(2)}, u32[]{:S(2)}) %collective-permute-start) | collective-permute-done | bytes 1310752 | tf_op jit(solution)/shard_map/ppermute | solution.py:434
  255.6 2.8 collective-permute-start.3
  258.4 3.7 %collective-permute-done.2.far_a = bf16[256,512]{1,0:T(8,128)(2,1)S(1)} collective-permute-done((bf16[256,512]{1,0:T(8,128)(2,1)S(1)}, bf16[256,512]{1,0:T(8,128)(2,1)S(1)}, u32[]{:S(2)}, u32[]{:S(2)}) %collective-permute-start.2) | collective-permute-done | bytes 262176 | tf_op jit(solution)/shard_map/ppermute | solution.py:436
  263.5 25.5 %ladder.1.base = f32[512,2048]{1,0:T(8,128)} custom-call(s32[1]{0:T(128)} %bitcast.2.me, bf16[512,2048]{1,0:T(8,128)(2,1)} %bitcast.9, bf16[1280,512]{1,0:T(8,128)(2,1)} %copy-done.6, bf16[1280,512]{1,0:T(8,128)(2,1)} %copy-done.7, bf16[256,512]{1,0:T(8,128)(2,1)} %copy-done.10, bf16[256,512]{1,0:T(8,128)(2,1)} %copy-done.11, f32[1,2048]{1,0:T(1,128)} %energy.5, ...), custom_call_target="tpu_custom_call" | custom-call | tf_op jit(solution)/shard_map/ladder/pallas_call | solution.py:171
  290.3 6.4 %finish.1 = f32[512,2048]{1,0:T(8,128)} custom-call(s32[4,16]{1,0:T(4,128)} %bitcast.12, s32[4,16]{1,0:T(4,128)} %bitcast.15, f32[512,2048]{1,0:T(8,128)} %ladder.1.base, bf16[64,128,128]{2,1,0:T(8,128)(2,1)} %copy-done.3, bf16[8,128,128]{2,1,0:T(8,128)(2,1)} %recoup.11), custom_call_target="tpu_custom_call" | custom-call | tf_op jit(solution)/shard_map/finish/pallas_call | solution.py:399
  (61 shorter events, 20.2 us)
Async XLA Ops:
  3.7 43.6 %all-to-all-start = ((bf16[64,72,128]{2,1,0:T(8,128)(2,1)}), bf16[64,72,128]{2,1,0:T(8,128)(2,1)S(1)}, u32[]{:S(2)}, u32[]{:S(2)}) async-start(bf16[64,72,128]{2,1,0:T(8,128)(2,1)} %shard_map.73), calls=%async_computation | async-start | bytes 2359296 | tf_op jit(solution)/shard_map/all_to_all | solution.py:431
  47.3 41.0 %copy-start = (bf16[64,72,128]{2,1,0:T(8,128)(2,1)}, bf16[64,72,128]{2,1,0:T(8,128)(2,1)S(1)}, u32[]{:S(2)}) copy-start(bf16[64,72,128]{2,1,0:T(8,128)(2,1)S(1)} %all-to-all-done.refs_0_.refs_3_.refs_1_) | copy-start | bytes 3538948
  47.3 34.9 %all-to-all-start.1 = ((bf16[64,64,128]{2,1,0:T(8,128)(2,1)}), bf16[64,64,128]{2,1,0:T(8,128)(2,1)}, u32[]{:S(2)}, u32[]{:S(2)}) async-start(bf16[64,64,128]{2,1,0:T(8,128)(2,1)} %shard_map.76), calls=%async_computation.1 | async-start | bytes 2097152 | tf_op jit(solution)/shard_map/all_to_all | solution.py:431
  54.1 57.7 %copy-start.12 = (s32[1,4,16]{2,1,0:T(4,128)S(1)}, s32[1,4,16]{2,1,0:T(4,128)}, u32[]{:S(2)}) copy-start(s32[1,4,16]{2,1,0:T(4,128)} %param.13) | copy-start | bytes 772
  54.1 30.8 %collective-permute-start.7 = (bf16[64,72,128]{2,1,0:T(8,128)(2,1)S(1)}, bf16[64,72,128]{2,1,0:T(8,128)(2,1)S(1)}, u32[]{:S(2)}, u32[]{:S(2)}) collective-permute-start(bf16[64,72,128]{2,1,0:T(8,128)(2,1)S(1)} %all-to-all-done.refs_0_.refs_3_.refs_1_), channel_id=1, source_target_pairs={{0,3},{1,0},{2,1},{3,2},{4,7},{5,4},{6,5},{7,6},{8,11},{9,8},{10,9... | collective-permute-start | bytes 3538952 | tf_op jit(solution)/shard_map/ppermute | solution.py:455
  56.9 30.4 %collective-permute-start.8 = (bf16[64,72,128]{2,1,0:T(8,128)(2,1)S(1)}, bf16[64,72,128]{2,1,0:T(8,128)(2,1)S(1)}, u32[]{:S(2)}, u32[]{:S(2)}) collective-permute-start(bf16[64,72,128]{2,1,0:T(8,128)(2,1)S(1)} %all-to-all-done.refs_0_.refs_3_.refs_1_), channel_id=1, source_target_pairs={{0,1},{1,2},{2,3},{3,0},{4,5},{5,6},{6,7},{7,4},{8,9},{9,10},{10,1... | collective-permute-start | bytes 3538952 | tf_op jit(solution)/shard_map/ppermute | solution.py:454
  82.2 25.1 %collective-permute-start.12 = (bf16[64,64,128]{2,1,0:T(8,128)(2,1)}, bf16[64,64,128]{2,1,0:T(8,128)(2,1)S(1)}, u32[]{:S(2)}, u32[]{:S(2)}) collective-permute-start(bf16[64,64,128]{2,1,0:T(8,128)(2,1)} %all-to-all-done.1.refs_0_), channel_id=1, source_target_pairs={{0,1},{1,2},{2,3},{3,0},{4,5},{5,6},{6,7},{7,4},{8,9},{9,10},{10,1... | collective-permute-start | bytes 3145736 | tf_op jit(solution)/shard_map/ppermute | solution.py:454
  83.5 24.7 %collective-permute-start.11 = (bf16[64,64,128]{2,1,0:T(8,128)(2,1)}, bf16[64,64,128]{2,1,0:T(8,128)(2,1)S(1)}, u32[]{:S(2)}, u32[]{:S(2)}) collective-permute-start(bf16[64,64,128]{2,1,0:T(8,128)(2,1)} %all-to-all-done.1.refs_0_), channel_id=1, source_target_pairs={{0,3},{1,0},{2,1},{3,2},{4,7},{5,4},{6,5},{7,6},{8,11},{9,8},{10,9... | collective-permute-start | bytes 3145736 | tf_op jit(solution)/shard_map/ppermute | solution.py:455
  84.9 24.2 %copy-start.1 = (bf16[64,72,128]{2,1,0:T(8,128)(2,1)}, bf16[64,72,128]{2,1,0:T(8,128)(2,1)S(1)}, u32[]{:S(2)}) copy-start(bf16[64,72,128]{2,1,0:T(8,128)(2,1)S(1)} %collective-permute-done.7.refs_1_.refs_4_.refs_2_) | copy-start | bytes 3538948
  85.8 91.4 %collective-permute-start.10 = (bf16[32,72,128]{2,1,0:T(8,128)(2,1)}, bf16[32,72,128]{2,1,0:T(8,128)(2,1)}, u32[]{:S(2)}, u32[]{:S(2)}) collective-permute-start(bf16[32,72,128]{2,1,0:T(8,128)(2,1)} %slice.27), channel_id=1, source_target_pairs={{0,3},{1,0},{2,1},{3,2},{4,7},{5,4},{6,5},{7,6},{8,11},{9,8},{10,9... | collective-permute-start | bytes 1769480 | tf_op jit(solution)/shard_map/ppermute | solution.py:456
  87.3 60.7 %copy-start.2 = (bf16[64,72,128]{2,1,0:T(8,128)(2,1)}, bf16[64,72,128]{2,1,0:T(8,128)(2,1)S(1)}, u32[]{:S(2)}) copy-start(bf16[64,72,128]{2,1,0:T(8,128)(2,1)S(1)} %collective-permute-done.8.refs_2_.refs_5_.refs_3_) | copy-start | bytes 3538948
  88.2 88.9 %collective-permute-start.9 = (bf16[32,72,128]{2,1,0:T(8,128)(2,1)}, bf16[32,72,128]{2,1,0:T(8,128)(2,1)}, u32[]{:S(2)}, u32[]{:S(2)}) collective-permute-start(bf16[32,72,128]{2,1,0:T(8,128)(2,1)} %slice.26), channel_id=1, source_target_pairs={{0,1},{1,2},{2,3},{3,0},{4,5},{5,6},{6,7},{7,4},{8,9},{9,10},{10,1... | collective-permute-start | bytes 1769480 | tf_op jit(solution)/shard_map/ppermute | solution.py:456
  108.2 76.6 %collective-permute-start.13 = (bf16[32,64,128]{2,1,0:T(8,128)(2,1)}, bf16[32,64,128]{2,1,0:T(8,128)(2,1)S(1)}, u32[]{:S(2)}, u32[]{:S(2)}) collective-permute-start(bf16[32,64,128]{2,1,0:T(8,128)(2,1)} %slice.28), channel_id=1, source_target_pairs={{0,1},{1,2},{2,3},{3,0},{4,5},{5,6},{6,7},{7,4},{8,9},{9,10},{10,1... | collective-permute-start | bytes 1572872 | tf_op jit(solution)/shard_map/ppermute | solution.py:456
  109.1 75.7 %collective-permute-start.14 = (bf16[32,64,128]{2,1,0:T(8,128)(2,1)}, bf16[32,64,128]{2,1,0:T(8,128)(2,1)S(1)}, u32[]{:S(2)}, u32[]{:S(2)}) collective-permute-start(bf16[32,64,128]{2,1,0:T(8,128)(2,1)} %slice.29), channel_id=1, source_target_pairs={{0,3},{1,0},{2,1},{3,2},{4,7},{5,4},{6,5},{7,6},{8,11},{9,8},{10,9... | collective-permute-start | bytes 1572872 | tf_op jit(solution)/shard_map/ppermute | solution.py:456
  111.8 19.1 %collective-permute-start.4 = (s32[4,16]{1,0:T(4,128)S(1)}, s32[4,16]{1,0:T(4,128)S(1)}, u32[]{:S(2)}, u32[]{:S(2)}) collective-permute-start(s32[4,16]{1,0:T(4,128)S(1)} %bitcast.17), channel_id=1, source_target_pairs={{0,3},{1,0},{2,1},{3,2},{4,7},{5,4},{6,5},{7,6},{8,11},{9,8},{10,9... | collective-permute-start | bytes 776 | tf_op jit(solution)/shard_map/ppermute | solution.py:440
  130.9 7.6 %copy-start.13 = (s32[4,16]{1,0:T(4,128)}, s32[4,16]{1,0:T(4,128)S(1)}, u32[]{:S(2)}) copy-start(s32[4,16]{1,0:T(4,128)S(1)} %collective-permute-done.4.right) | copy-start | bytes 772
  130.9 3.9 %collective-permute-start.5 = (s32[4,16]{1,0:T(4,128)S(1)}, s32[4,16]{1,0:T(4,128)S(1)}, u32[]{:S(2)}, u32[]{:S(2)}) collective-permute-start(s32[4,16]{1,0:T(4,128)S(1)} %bitcast.18), channel_id=1, source_target_pairs={{0,2},{1,3},{2,0},{3,1},{4,6},{5,7},{6,4},{7,5},{8,10},{9,11},{10,... | collective-permute-start | bytes 776 | tf_op jit(solution)/shard_map/ppermute | solution.py:441
  134.8 3.7 %collective-permute-start.6 = (s32[4,16]{1,0:T(4,128)S(1)}, s32[4,16]{1,0:T(4,128)S(1)}, u32[]{:S(2)}, u32[]{:S(2)}) collective-permute-start(s32[4,16]{1,0:T(4,128)S(1)} %bitcast.19), channel_id=1, source_target_pairs={{0,1},{1,2},{2,3},{3,0},{4,5},{5,6},{6,7},{7,4},{8,9},{9,10},{10,1... | collective-permute-start | bytes 776 | tf_op jit(solution)/shard_map/ppermute | solution.py:442
  208.4 80.6 %all-to-all-start.2 = ((bf16[64,128,128]{2,1,0:T(8,128)(2,1)}), bf16[64,128,128]{2,1,0:T(8,128)(2,1)S(1)}, u32[]{:S(2)}, u32[]{:S(2)}) async-start(bf16[64,128,128]{2,1,0:T(8,128)(2,1)} %cross.1), calls=%async_computation.2 | async-start | bytes 4194304 | tf_op jit(solution)/shard_map/all_to_all | solution.py:466
  222.9 31.3 %collective-permute-start = (bf16[1280,512]{1,0:T(8,128)(2,1)}, bf16[1280,512]{1,0:T(8,128)(2,1)S(1)}, u32[]{:S(2)}, u32[]{:S(2)}) collective-permute-start(bf16[1280,512]{1,0:T(8,128)(2,1)} %get-tuple-element.15), channel_id=1, source_target_pairs={{0,1},{1,2},{2,3},{3,0},{4,5},{5,6},{6,7},{7,4},{8,9},{9,10},{10,1... | collective-permute-start | bytes 3932168 | tf_op jit(solution)/shard_map/ppermute | solution.py:434
  222.9 31.4 %collective-permute-start.1 = (bf16[1280,512]{1,0:T(8,128)(2,1)}, bf16[1280,512]{1,0:T(8,128)(2,1)S(1)}, u32[]{:S(2)}, u32[]{:S(2)}) collective-permute-start(bf16[1280,512]{1,0:T(8,128)(2,1)} %get-tuple-element.16), channel_id=1, source_target_pairs={{0,3},{1,0},{2,1},{3,2},{4,7},{5,4},{6,5},{7,6},{8,11},{9,8},{10,9... | collective-permute-start | bytes 3932168 | tf_op jit(solution)/shard_map/ppermute | solution.py:435
  254.2 8.3 %copy-start.6 = (bf16[1280,512]{1,0:T(8,128)(2,1)}, bf16[1280,512]{1,0:T(8,128)(2,1)S(1)}, u32[]{:S(2)}) copy-start(bf16[1280,512]{1,0:T(8,128)(2,1)S(1)} %collective-permute-done.from_left) | copy-start | bytes 3932164
  254.3 7.8 %collective-permute-start.2 = (bf16[256,512]{1,0:T(8,128)(2,1)S(1)}, bf16[256,512]{1,0:T(8,128)(2,1)S(1)}, u32[]{:S(2)}, u32[]{:S(2)}) collective-permute-start(bf16[256,512]{1,0:T(8,128)(2,1)S(1)} %slice.24), channel_id=1, source_target_pairs={{0,1},{1,2},{2,3},{3,0},{4,5},{5,6},{6,7},{7,4},{8,9},{9,10},{10,1... | collective-permute-start | bytes 786440 | tf_op jit(solution)/shard_map/ppermute | solution.py:436
  255.6 6.9 %collective-permute-start.3 = (bf16[256,512]{1,0:T(8,128)(2,1)S(1)}, bf16[256,512]{1,0:T(8,128)(2,1)S(1)}, u32[]{:S(2)}, u32[]{:S(2)}) collective-permute-start(bf16[256,512]{1,0:T(8,128)(2,1)S(1)} %slice.25), channel_id=1, source_target_pairs={{0,3},{1,0},{2,1},{3,2},{4,7},{5,4},{6,5},{7,6},{8,11},{9,8},{10,9... | collective-permute-start | bytes 786440 | tf_op jit(solution)/shard_map/ppermute | solution.py:437
  (10 other events, 18.2 us)

commit v2 on v1

--- a/solution.py
+++ b/solution.py
@@ -17,7 +17,7 @@
 ROWS = TB // CHUNKS
 SMEM = pl.BlockSpec(memory_space=pltpu.SMEM)
 VMEM = pl.BlockSpec(memory_space=pltpu.VMEM)
-ANY = pl.BlockSpec(memory_space=pl.ANY)
+ANY = pl.BlockSpec(memory_space=pltpu.HBM)
 BIG = pltpu.CompilerParams(vmem_limit_bytes=60 << 20)
 
 
@@ -67,17 +67,23 @@
 
 
 def tables_kernel(own, right, far, left, out):
+    across = own.shape[1]
     for n, table in enumerate((own, right, far, left)):
-        out[n] = table[...]
-
-
-def join_tables(*tables):
+
+        def body(p, carry, n=n, table=table):
+            out[n, table[p // across, p % across]] = p
+            return carry
+
+        lax.fori_loop(0, own.shape[0] * across, body, 0, unroll=8)
+
+
+def place_tables(*tables):
     return pl.pallas_call(
         tables_kernel,
-        out_shape=jax.ShapeDtypeStruct((4,) + tables[0].shape, jnp.int32),
-        in_specs=[VMEM] * 4,
-        out_specs=VMEM,
-        name="join_tables",
+        out_shape=jax.ShapeDtypeStruct((4, tables[0].size), jnp.int32),
+        in_specs=[SMEM] * 4,
+        out_specs=SMEM,
+        name="place_tables",
     )(*tables)
 
 
@@ -183,18 +189,6 @@
     )(me, gamma, from_left, from_right, far_a, far_b, energy, occ)
 
 
-def decode(head, picks, down, along, cls, cls_int, sem):
-    count = down.shape[1]
-    lines = jnp.dot(picks[...], head, preferred_element_type=F32)
-    side = jnp.concatenate([lines[0:count], jnp.zeros((TB - count, TB), F32)], axis=0) if count < TB else lines[0:count]
-    down[...] = jnp.transpose(side)[:, 0:count]
-    along[...] = lines[count : 2 * count]
-    cls_int[...] = lines[2 * count :].astype(jnp.int32)
-    copy = pltpu.make_async_copy(cls_int, cls, sem)
-    copy.start()
-    copy.wait()
-
-
 def fill_picks(picks, count):
     row = lax.broadcasted_iota(jnp.int32, picks.shape, 0)
     col = lax.broadcasted_iota(jnp.int32, picks.shape, 1)
@@ -203,107 +197,130 @@
     picks[...] = jnp.where((col // META == row % count) & hit, 1.0, 0.0).astype(BF)
 
 
-def recouple_block(chunk, across, raw, block, recv, recoup, scratch, put):
-    down, along, cls, eta = scratch
+def decode(head, picks, down, along, cls):
+    count = along.shape[0]
+    lines = jnp.dot(picks[...], head, preferred_element_type=F32)
+    turned = jnp.transpose(jnp.concatenate([lines[0:count], lines[2 * count :]], axis=0))
+    down[...] = turned
+    along[...] = lines[count : 2 * count]
+    cls[...] = turned[0:META].astype(jnp.int32)
+
+
+def recouple_block(chunk, across, raw, down, along, cls, places, block, recoup, put):
     count = raw.shape[0]
     for q in range(count):
         column = down[chunk * ROWS : (chunk + 1) * ROWS, q : q + 1]
         line = along[q : q + 1, :]
-        ratio = raw[q].astype(F32) / (column - line)
-        eta[q] = jnp.where(column * line < 0.0, ratio, 0.0).astype(BF)
-
-    def body(p, carry):
-        i, j = p // across, p % across
-        q = recv[block, i, j]
-        both = jnp.concatenate([eta[q], raw[q]], axis=0)
-        done = jnp.dot(both, recoup[cls[q, 0]], preferred_element_type=F32).astype(BF)
-        put(i, pl.ds(pl.multiple_of(j * TB, TB), TB), done[0:ROWS], done[ROWS:])
-        return carry
-
-    lax.fori_loop(0, count, body, 0, unroll=8)
-
-
-def block_scratch(groups, count):
-    return [
-        pltpu.VMEM((groups, count, ROWS, TB), BF),
-        pltpu.VMEM((groups, count, META, TB), BF),
-        pltpu.VMEM((3 * count, count * META), BF),
-        pltpu.VMEM((TB, count), F32),
-        pltpu.VMEM((count, TB), F32),
-        pltpu.VMEM((count, TB), jnp.int32),
-        pltpu.SMEM((count, TB), jnp.int32),
-        pltpu.VMEM((count, ROWS, TB), BF),
-        pltpu.SemaphoreType.DMA((groups, 5)),
-    ]
-
-
-def waits(raws, heads, raw, head, sems):
+        tile = raw[q]
+        ratio = tile.astype(F32) / (column - line)
+        eta = jnp.where(column * line < 0.0, ratio, 0.0).astype(BF)
+        both = jnp.concatenate([eta, tile], axis=0)
+        done = jnp.dot(both, recoup[cls(q)], preferred_element_type=F32).astype(BF)
+        p = places[block, q]
+        put(p // across, pl.ds(pl.multiple_of((p % across) * TB, TB), TB), done[0:ROWS], done[ROWS:])
+
+
+def body_copies(raws, raw, sems):
     copies, start = [], 0
-    for n, (source, top) in enumerate(zip(raws, heads)):
+    for n, source in enumerate(raws):
         where = pl.ds(start, source.shape[0])
         start += source.shape[0]
-        copies.append(pltpu.make_async_copy(top.at[:, ROWS : ROWS + META, :], head.at[where], sems.at[2 * n + 1]))
-        copies.append(pltpu.make_async_copy(source.at[:, 0:ROWS, :], raw.at[where], sems.at[2 * n]))
+        copies.append(pltpu.make_async_copy(source.at[:, 0:ROWS, :], raw.at[where], sems.at[n]))
     return copies
 
 
-def fetch(*refs):
-    copies = waits(*refs)
-    for copy in copies:
+def head_copies(raws, head, sems):
+    copies, start = [], 0
+    for n, source in enumerate(raws):
+        where = pl.ds(start, source.shape[0])
+        start += source.shape[0]
+        copies.append(pltpu.make_async_copy(source.at[:, ROWS : ROWS + META, :], head.at[where], sems.at[n]))
+    return copies
+
+
+def recouple_kernel(chunk, across, parts, blocks, places, recoup, *refs):
+    groups = len(blocks)
+    total = parts * groups
+    raws, refs = refs[:total], refs[total:]
+    if chunk == 0:
+        eta_out, gamma_out, down, along, cls_int, raw, sems, head, picks, cls, head_sems = refs
+    else:
+        down, along, cls, eta_out, gamma_out, raw, sems = refs
+    for n in range(groups):
+        mine = raws[n * parts : (n + 1) * parts]
+        if chunk == 0:
+            for copy in head_copies(mine, head.at[n], head_sems.at[n]):
+                copy.start()
+        for copy in body_copies(mine, raw.at[n], sems.at[n]):
+            copy.start()
+    count = raw.shape[1]
+    high = eta_out.shape[0] // groups
+    if chunk == 0:
+        fill_picks(picks, count)
+        for n in range(groups):
+            for copy in head_copies(raws[n * parts : (n + 1) * parts], head.at[n], head_sems.at[n]):
+                copy.wait()
+            decode(head[n].reshape(count * META, TB), picks, down.at[n], along.at[n], cls_int.at[n])
+        copy = pltpu.make_async_copy(cls_int, cls, head_sems.at[0, 0])
         copy.start()
-    return copies
-
-
-def recouple_kernel(chunk, across, parts, blocks, recv, recoup, *refs):
-    total = parts * len(blocks)
-    raws, heads, refs = refs[:total], refs[total : 2 * total], refs[2 * total :]
-    eta_out, gamma_out, raw, head, picks, down, along, cls_int, cls, eta, sems = refs
-    for n in range(len(blocks)):
-        span = slice(n * parts, (n + 1) * parts)
-        fetch(raws[span], heads[span], raw.at[n], head.at[n], sems.at[n])
-    count = raw.shape[1]
-    high = eta_out.shape[0] // len(blocks)
-    fill_picks(picks, count)
+        copy.wait()
 
     def group(n, carry):
         block = sum(jnp.where(n == k, b, 0) for k, b in enumerate(blocks))
-        for copy in waits(raws[:parts], heads[:parts], raw.at[n], head.at[n], sems.at[n]):
+        for copy in body_copies(raws[:parts], raw.at[n], sems.at[n]):
             copy.wait()
-        decode(head[n].reshape(count * META, TB), picks, down, along, cls, cls_int, sems.at[n, 4])
 
         def put(i, cols, eta_tile, gamma_tile):
             eta_out[n * high + i, :, cols] = eta_tile
             gamma_out[n * high + i, :, cols] = gamma_tile
 
-        recouple_block(chunk, across, raw.at[n], block, recv, recoup, (down, along, cls, eta), put)
+        recouple_block(
+            chunk, across, raw.at[n], down.at[n], along.at[n], lambda q: cls[n, 0, count + q], places, block, recoup, put
+        )
         return carry
 
-    lax.fori_loop(0, len(blocks), group, 0)
-
-
-def recouple(chunk, across, blocks, tables, recoup, raws, heads):
-    parts = len(raws[0])
+    lax.fori_loop(0, groups, group, 0)
+
+
+def recouple(chunk, across, blocks, places, recoup, raws, codes):
+    groups, parts = len(blocks), len(raws[0])
     count = sum(raw.shape[0] for raw in raws[0])
-    shape = jax.ShapeDtypeStruct((len(blocks) * count // across, ROWS, across * TB), BF)
-    return pl.pallas_call(
+    shapes = [jax.ShapeDtypeStruct((groups * count // across, ROWS, across * TB), BF)] * 2
+    in_specs = [SMEM, VMEM] + [ANY] * (parts * groups)
+    scratch = [pltpu.VMEM((groups, count, ROWS, TB), BF), pltpu.SemaphoreType.DMA((groups, parts))]
+    if chunk == 0:
+        shapes += [
+            jax.ShapeDtypeStruct((groups, TB, 2 * count), F32),
+            jax.ShapeDtypeStruct((groups, count, TB), F32),
+            jax.ShapeDtypeStruct((groups, META, 2 * count), jnp.int32),
+        ]
+        scratch += [
+            pltpu.VMEM((groups, count, META, TB), BF),
+            pltpu.VMEM((3 * count, count * META), BF),
+            pltpu.SMEM((groups, META, 2 * count), jnp.int32),
+            pltpu.SemaphoreType.DMA((groups, parts)),
+        ]
+    else:
+        in_specs += [VMEM, VMEM, SMEM]
+    outs = pl.pallas_call(
         functools.partial(recouple_kernel, chunk, across, parts, blocks),
-        out_shape=[shape, shape],
-        in_specs=[SMEM, VMEM] + [ANY] * (2 * parts * len(blocks)),
-        out_specs=[VMEM, VMEM],
-        scratch_shapes=block_scratch(len(blocks), count),
+        out_shape=shapes,
+        in_specs=in_specs,
+        out_specs=[VMEM] * len(shapes),
+        scratch_shapes=scratch,
         compiler_params=BIG,
-    )(tables, recoup, *[r for group in raws for r in group], *[r for group in heads for r in group])
-
-
-def cross_kernel(chunk, blocks, parts, me, recv, recoup, *refs):
+    )(places, recoup, *[r for group in raws for r in group], *codes)
+    return outs[0:2], outs[2:]
+
+
+def cross_kernel(chunk, blocks, parts, me, recv, places, cls, recoup, down, along, *refs):
     groups = len(set(key for _, _, key, _ in blocks))
     pieces, refs = refs[: 2 * groups], refs[2 * groups :]
-    raws, heads, refs = refs[:parts], refs[parts : 2 * parts], refs[2 * parts :]
-    out, eta, gamma, turned, piece_sems = refs[:5]
-    raw, head, picks, down, along, cls_int, cls, eta_raw, sems = refs[5:]
-    rows_down = recv.shape[1]
+    raws, refs = refs[:parts], refs[parts:]
+    out, eta, gamma, turned, piece_sems, raw, sems = refs
+    rows_down = recv.shape[0]
     width = pieces[0].shape[2]
-    late = fetch(raws, heads, raw.at[0], head.at[0], sems.at[0])
+    late = body_copies(raws, raw, sems)
     copies = []
     for n, (part, block, key, place) in enumerate(blocks):
         where = pl.ds(((me[0] + block) % 4) * rows_down, rows_down)
@@ -311,20 +328,20 @@
             source = pieces[2 * key + which].at[pl.ds(place * rows_down, rows_down)]
             into = target.at[where, pl.ds(part * ROWS, ROWS), :]
             copies.append(pltpu.make_async_copy(source, into, piece_sems.at[2 * n + which]))
-    for copy in copies:
+    for copy in late + copies:
         copy.start()
-    count = raw.shape[1]
-    fill_picks(picks, count)
     for copy in late:
         copy.wait()
-    decode(head[0].reshape(count * META, TB), picks, down, along, cls, cls_int, sems.at[0, 4])
+    count = raw.shape[0]
     far = ((me[0] + 2) % 4) * rows_down
 
     def put(i, cols, eta_tile, gamma_tile):
         eta[far + i, chunk * ROWS : (chunk + 1) * ROWS, cols] = eta_tile
         gamma[far + i, chunk * ROWS : (chunk + 1) * ROWS, cols] = gamma_tile
 
-    recouple_block(chunk, width // TB, raw.at[0], 2, recv, recoup, (down, along, cls, eta_raw), put)
+    recouple_block(
+        chunk, width // TB, raw, down.at[0], along.at[0], lambda q: cls[0, 0, count + q], places, 2, recoup, put
+    )
     for copy in copies:
         copy.wait()
     side = rows_down * TB
@@ -352,64 +369,81 @@
         result = (half - other).astype(BF)
         for i in range(rows_down):
             for j in range(step):
-                out[recv[0, i, n * step + j]] = result[i * TB : (i + 1) * TB, j * TB : (j + 1) * TB]
+                out[recv[i, n * step + j]] = result[i * TB : (i + 1) * TB, j * TB : (j + 1) * TB]
         return carry
 
     lax.fori_loop(0, width // (step * TB), body, 0)
 
 
-def cross(chunk, me, tables, recoup, pieces, raws, heads):
+def cross(chunk, me, recv, places, recoup, pieces, raws, codes):
     flat = [array for _, _, pair in pieces for array in pair]
     blocks = tuple(
         (part, block, key, place)
         for key, (part, members, _) in enumerate(pieces)
         for place, block in enumerate(members)
     )
-    rows_down, width = tables.shape[1], flat[0].shape[2]
+    rows_down, width = recv.shape[0], flat[0].shape[2]
+    down, along, cls = codes
     return pl.pallas_call(
         functools.partial(cross_kernel, chunk, blocks, len(raws)),
-        out_shape=jax.ShapeDtypeStruct((tables[0].size, TB, TB), BF),
-        in_specs=[SMEM] * 2 + [VMEM] + [ANY] * (len(flat) + 2 * len(raws)),
+        out_shape=jax.ShapeDtypeStruct((recv.size, TB, TB), BF),
+        in_specs=[SMEM] * 4 + [VMEM] * 3 + [ANY] * (len(flat) + len(raws)),
         out_specs=VMEM,
         scratch_shapes=[
             pltpu.VMEM((4 * rows_down, TB, width), BF),
             pltpu.VMEM((4 * rows_down, TB, width), BF),
             pltpu.VMEM((rows_down * TB, width), BF),
             pltpu.SemaphoreType.DMA((2 * len(blocks),)),
-        ]
-        + block_scratch(1, tables[0].size),
+            pltpu.VMEM((recv.size, ROWS, TB), BF),
+            pltpu.SemaphoreType.DMA((len(raws),)),
+        ],
         compiler_params=BIG,
         name="cross",
-    )(me, tables, recoup, *flat, *raws, *heads)
-
-
-def final_kernel(step_size, send, cls, base, back, recoup, out):
-    i = pl.program_id(0)
-    for j in range(base.shape[1] // TB):
-        cols = slice(j * TB, (j + 1) * TB)
-        turned = lax.dot_general(
-            back[send[i, j]], recoup[cls[i, j]], (((1,), (1,)), ((), ())), preferred_element_type=F32
-        )
-        out[:, cols] = base[:, cols] + step_size * turned
+    )(me, recv, places, cls, recoup, down, along, *flat, *raws)
+
+
+def final_kernel(step_size, send, cls, recoup, base, back, out, total, tiles, sems, out_sems):
+    rows_down, across = send.shape
+    arrive = pltpu.make_async_copy(back, tiles, sems.at[rows_down])
+    arrive.start()
+    copies, leaves = [], []
+    for i in range(rows_down):
+        rows = pl.ds(i * TB, TB)
+        copies.append(pltpu.make_async_copy(base.at[rows], total.at[rows], sems.at[i]))
+        leaves.append(pltpu.make_async_copy(total.at[rows], out.at[rows], out_sems.at[i]))
+    for copy in copies:
+        copy.start()
+    arrive.wait()
+    for i in range(rows_down):
+        copies[i].wait()
+        rows = slice(i * TB, (i + 1) * TB)
+        for j in range(across):
+            cols = slice(j * TB, (j + 1) * TB)
+            turned = lax.dot_general(
+                tiles[send[i, j]], recoup[cls[i, j]], (((1,), (1,)), ((), ())), preferred_element_type=F32
+            )
+            total[rows, cols] = total[rows, cols] + step_size * turned
+        leaves[i].start()
+    for leave in leaves:
+        leave.wait()
 
 
 def finish(step_size, send, cls, base, back, recoup):
-    width = base.shape[1]
-    rows = pl.BlockSpec((TB, width), lambda i: (i, 0))
+    rows_down = send.shape[0]
     return pl.pallas_call(
         functools.partial(final_kernel, step_size),
-        grid=(base.shape[0] // TB,),
         out_shape=jax.ShapeDtypeStruct(base.shape, F32),
-        in_specs=[
-            SMEM,
-            SMEM,
-            rows,
-            pl.BlockSpec(back.shape, lambda i: (0, 0, 0)),
-            pl.BlockSpec(recoup.shape, lambda i: (0, 0, 0)),
+        in_specs=[SMEM, SMEM, VMEM, ANY, ANY],
+        out_specs=ANY,
+        scratch_shapes=[
+            pltpu.VMEM(base.shape, F32),
+            pltpu.VMEM(back.shape, BF),
+            pltpu.SemaphoreType.DMA((rows_down + 1,)),
+            pltpu.SemaphoreType.DMA((rows_down,)),
         ],
-        out_specs=rows,
+        compiler_params=BIG,
         name="finish",
-    )(send, cls, base, back, recoup)
+    )(send, cls, recoup, base, back)
 
 
 RIGHT = [(i, (i + 1) % 4) for i in range(4)]
@@ -435,7 +469,7 @@
     from_right = lax.ppermute(to_left, "tile", LEFT)
     far_a = lax.ppermute(from_left[0:half], "tile", RIGHT)
     far_b = lax.ppermute(from_right[half : 2 * half], "tile", LEFT)
-    tables = join_tables(
+    places = place_tables(
         recv,
         lax.ppermute(recv, "tile", LEFT),
         lax.ppermute(recv, "tile", ACROSS),
@@ -443,10 +477,12 @@
     )
     base = ladder_base(step_size, me, gamma, from_left, from_right, far_a, far_b, energies, occupancy)
 
-    pieces, heads = [], None
-
-    def form(chunk, members, raws, tops):
-        pieces.append((chunk, members, recouple(chunk, across, members, tables, recoup, raws, tops)))
+    pieces, codes = [], {}
+
+    def form(kind, chunk, members, raws):
+        pair, code = recouple(chunk, across, members, places, recoup, raws, codes.get(kind, ()))
+        pieces.append((chunk, members, pair))
+        codes.setdefault(kind, code)
 
     for h in range(CHUNKS):
         own = arrived[h]
@@ -454,15 +490,11 @@
         left = lax.ppermute(own, "tile", RIGHT)
         right = lax.ppermute(own, "tile", LEFT)
         opposite = [lax.ppermute(left[0:mid], "tile", RIGHT), lax.ppermute(right[mid:], "tile", LEFT)]
-        if h == 0:
-            heads = ([own], [right], opposite, [left])
+        form("own", h, (0,), ([own],))
+        form("side", h, (1, 3), ([right], [left]))
         if h + 1 < CHUNKS:
-            form(h, (0, 1, 3), ([own], [right], [left]), (heads[0], heads[1], heads[3]))
-            form(h, (2,), (opposite,), (heads[2],))
-        else:
-            form(h, (0,), ([own],), (heads[0],))
-            form(h, (1, 3), ([right], [left]), (heads[1], heads[3]))
-    crossed = cross(CHUNKS - 1, me, tables, recoup, pieces, opposite, heads[2])
+            form("far", h, (2,), (opposite,))
+    crossed = cross(CHUNKS - 1, me, recv, places, recoup, pieces, opposite, codes["far"])
     back = lax.all_to_all(crossed, "chan", split_axis=0, concat_axis=0, tiled=True)
     return finish(step_size, send, cls, base, back, recoup)[None]
 

time: 299 us -> 284 us (0.950)
  Pallas kernels: 110 us -> 93.5 us
    ppermute x1, waiting for transfers between devices: 18.9 us -> 1.3 us  [on_device(): lax.ppermute(recv, 'tile', LEFT)]
    ppermute x1, waiting for transfers between devices: 2.39 us -> 19.3 us  [on_device(): lax.ppermute(recv, 'tile', RIGHT)]
    pallas_call x4 -> x5, Pallas kernels: 44.3 us -> 28.3 us  [recouple(): pl.pallas_call(functools.partial(recouple_kernel, chunk, across, parts, b...]
  transfers between devices with their start and end apart: 18 -> 18, of which waited for: 9 -> 9; matrix products, arithmetic and copies ran while one was open for 1% -> 2% of each run, Pallas kernels for 26% -> 23%
where the time goes in v2:
time: 284 us; the launch traced here: 281 us
  waiting for transfers between devices  126 us (44%)
  Pallas kernels  93.5 us (33%)
  starting transfers between devices  51.7 us (18%)
  local copies, waits for them, and re-layouts  9.89 us (3%)
    all_to_all x2, waiting for transfers between devices, on_device(): lax.all_to_all(buf, 'chan', split_axis=0, concat_axis=0, tiled=True)  52.5 us
    ppermute x1, waiting for transfers between devices, on_device(): from_left = lax.ppermute(to_right, 'tile', RIGHT)  28.6 us
    pallas_call x5, Pallas kernels, recouple(): pl.pallas_call(functools.partial(recouple_kernel, chunk, across, parts, b...  28.3 us
    pallas_call x1, Pallas kernels, ladder_base(): pl.pallas_call(functools.partial(ladder_kernel, step_size), out_shape=jax...  25.5 us
    pallas_call x1, Pallas kernels, cross(): pl.pallas_call(functools.partial(cross_kernel, chunk, blocks, len(raws)),...  19.9 us
    all_to_all x2, starting transfers between devices, on_device(): lax.all_to_all(buf, 'chan', split_axis=0, concat_axis=0, tiled=True)  19.6 us
    ppermute x1, waiting for transfers between devices, on_device(): lax.ppermute(recv, 'tile', RIGHT)  19.3 us
    ppermute x2, waiting for transfers between devices, on_device(): left = lax.ppermute(own, 'tile', RIGHT)  17.8 us
  transfers between devices with their start and end apart: 18, of which 9 were waited for; matrix products, arithmetic and copies ran while one was open for 2% of the time, Pallas kernels for 23%

profile of v2, /device:TPU:1, one launch (start us, length us, event | category | flops | bytes accessed | tf_op | source)
XLA Modules:
  0.0 281.5 jit_solution(10974403671281032493)
XLA Ops:
  0.0 3.7 %shard_map.73 = bf16[64,72,128]{2,1,0:T(8,128)(2,1)} custom-call(s32[1]{0:T(128)} %bitcast.2.me, s32[4,16]{1,0:T(4,128)} %bitcast.10, s32[4,16]{1,0:T(4,128)} %bitcast.13, bf16[512,2048]{1,0:T(8,128)(2,1)} %bitcast.6, f32[1,2048]{1,0:T(1,128)} %energy.5, s32[1,2048]{1,0:T(1,128)} %occ.5), custom_call_target="tpu_custom_call" | custom-call | tf_op jit(solution)/shard_map/pallas_call | solution.py:60
  3.7 13.0 %all-to-all-start = ((bf16[64,72,128]{2,1,0:T(8,128)(2,1)}), bf16[64,72,128]{2,1,0:T(8,128)(2,1)S(1)}, u32[]{:S(2)}, u32[]{:S(2)}) async-start(bf16[64,72,128]{2,1,0:T(8,128)(2,1)} %shard_map.73), calls=%async_computation | async-start | bytes 2359296 | tf_op jit(solution)/shard_map/all_to_all | solution.py:465
  16.7 3.5 %shard_map.77 = bf16[64,64,128]{2,1,0:T(8,128)(2,1)} custom-call(s32[1]{0:T(128)} %bitcast.2.me, s32[4,16]{1,0:T(4,128)} %bitcast.11, s32[4,16]{1,0:T(4,128)} %bitcast.14, bf16[512,2048]{1,0:T(8,128)(2,1)} %bitcast.7, f32[1,2048]{1,0:T(1,128)} %energy.5, s32[1,2048]{1,0:T(1,128)} %occ.5), custom_call_target="tpu_custom_call" | custom-call | tf_op jit(solution)/shard_map/pallas_call | solution.py:60
  20.1 27.1 %all-to-all-done.refs_0_ = bf16[64,72,128]{2,1,0:T(8,128)(2,1)S(1)} async-done(((bf16[64,72,128]{2,1,0:T(8,128)(2,1)}), bf16[64,72,128]{2,1,0:T(8,128)(2,1)S(1)}, u32[]{:S(2)}, u32[]{:S(2)}) %all-to-all-start) | async-done | bytes 1179680 | tf_op jit(solution)/shard_map/all_to_all | solution.py:465
  47.3 6.6 %all-to-all-start.1 = ((bf16[64,64,128]{2,1,0:T(8,128)(2,1)}), bf16[64,64,128]{2,1,0:T(8,128)(2,1)S(1)}, u32[]{:S(2)}, u32[]{:S(2)}) async-start(bf16[64,64,128]{2,1,0:T(8,128)(2,1)} %shard_map.77), calls=%async_computation.1 | async-start | bytes 2097152 | tf_op jit(solution)/shard_map/all_to_all | solution.py:465
  53.9 2.8 collective-permute-start.9
  56.7 25.3 %all-to-all-done.1.refs_0_ = bf16[64,64,128]{2,1,0:T(8,128)(2,1)S(1)} async-done(((bf16[64,64,128]{2,1,0:T(8,128)(2,1)}), bf16[64,64,128]{2,1,0:T(8,128)(2,1)S(1)}, u32[]{:S(2)}, u32[]{:S(2)}) %all-to-all-start.1) | async-done | bytes 1048608 | tf_op jit(solution)/shard_map/all_to_all | solution.py:465
  89.2 17.8 %collective-permute-done.12.refs_1_ = bf16[64,64,128]{2,1,0:T(8,128)(2,1)S(1)} collective-permute-done((bf16[64,64,128]{2,1,0:T(8,128)(2,1)S(1)}, bf16[64,64,128]{2,1,0:T(8,128)(2,1)S(1)}, u32[]{:S(2)}, u32[]{:S(2)}) %collective-permute-start.12) | collective-permute-done | bytes 1048608 | tf_op jit(solution)/shard_map/ppermute | solution.py:490
  111.6 19.3 %collective-permute-done.6.left = s32[4,16]{1,0:T(4,128)S(1)} collective-permute-done((s32[4,16]{1,0:T(4,128)S(1)}, s32[4,16]{1,0:T(4,128)S(1)}, u32[]{:S(2)}, u32[]{:S(2)}) %collective-permute-start.6) | collective-permute-done | bytes 288 | tf_op jit(solution)/shard_map/ppermute | solution.py:476
  138.1 3.7 %place_tables.1.places = s32[4,64]{1,0:T(4,128)} custom-call(s32[4,16]{1,0:T(4,128)} %bitcast.16, s32[4,16]{1,0:T(4,128)} %copy-done.15, s32[4,16]{1,0:T(4,128)} %copy-done.14, s32[4,16]{1,0:T(4,128)} %copy-done.13), custom_call_target="tpu_custom_call" | custom-call | tf_op jit(solution)/shard_map/place_tables/pallas_call | solution.py:81
  141.8 5.0 %shard_map.75 = (bf16[4,64,2048]{2,1,0:T(8,128)(2,1)}, bf16[4,64,2048]{2,1,0:T(8,128)(2,1)}, f32[1,128,128]{2,1,0:T(8,128)}, f32[1,64,128]{2,1,0:T(8,128)}, s32[1,8,128]{2,1,0:T(8,128)}) custom-call(s32[4,64]{1,0:T(4,128)} %place_tables.1.places, bf16[8,128,128]{2,1,0:T(8,128)(2,1)} %recoup.13, bf16[64,72,128]{2,1,0:T(8,128)(2,1)} %copy-done.1), custom_call_target="tpu_custom_call" | custom-call | tf_op jit(solution)/shard_map/pallas_call | solution.py:305
  146.8 4.5 %shard_map.78 = (bf16[4,64,2048]{2,1,0:T(8,128)(2,1)}, bf16[4,64,2048]{2,1,0:T(8,128)(2,1)}) custom-call(s32[4,64]{1,0:T(4,128)} %place_tables.1.places, bf16[8,128,128]{2,1,0:T(8,128)(2,1)} %recoup.13, bf16[64,64,128]{2,1,0:T(8,128)(2,1)} %copy-done.2, f32[1,128,128]{2,1,0:T(8,128)} %get-tuple-element.37.refs_1_, f32[1,64,128]{2,1,0:T(8,128)} %get-tuple-element.38.refs_2_, ...), custom_call_target="tpu_custom_call" | custom-call | tf_op jit(solution)/shard_map/pallas_call | solution.py:305
  151.3 7.4 %shard_map.76 = (bf16[8,64,2048]{2,1,0:T(8,128)(2,1)}, bf16[8,64,2048]{2,1,0:T(8,128)(2,1)}, f32[2,128,128]{2,1,0:T(8,128)}, f32[2,64,128]{2,1,0:T(8,128)}, s32[2,8,128]{2,1,0:T(8,128)}) custom-call(s32[4,64]{1,0:T(4,128)} %place_tables.1.places, bf16[8,128,128]{2,1,0:T(8,128)(2,1)} %recoup.13, bf16[64,72,128]{2,1,0:T(8,128)(2,1)} %copy-done.3, ...), custom_call_target="tpu_custom_call" | custom-call | tf_op jit(solution)/shard_map/pallas_call | solution.py:305
  158.6 6.3 %shard_map.79 = (bf16[8,64,2048]{2,1,0:T(8,128)(2,1)}, bf16[8,64,2048]{2,1,0:T(8,128)(2,1)}) custom-call(s32[4,64]{1,0:T(4,128)} %place_tables.1.places, bf16[8,128,128]{2,1,0:T(8,128)(2,1)} %recoup.13, bf16[64,64,128]{2,1,0:T(8,128)(2,1)} %copy-done.5, bf16[64,64,128]{2,1,0:T(8,128)(2,1)} %copy-done.4, f32[2,128,128]{2,1,0:T(8,128)} %get-tuple-element.42.refs_2_, ...), custom_call_target="tpu_custom_call" | custom-call | tf_op jit(solution)/shard_map/pallas_call | solution.py:305
  165.0 5.1 %shard_map.74 = (bf16[4,64,2048]{2,1,0:T(8,128)(2,1)}, bf16[4,64,2048]{2,1,0:T(8,128)(2,1)}, f32[1,128,128]{2,1,0:T(8,128)}, f32[1,64,128]{2,1,0:T(8,128)}, s32[1,8,128]{2,1,0:T(8,128)}) custom-call(s32[4,64]{1,0:T(4,128)} %place_tables.1.places, bf16[8,128,128]{2,1,0:T(8,128)(2,1)} %recoup.13, bf16[32,72,128]{2,1,0:T(8,128)(2,1)} %collective-permute-done.8.refs_0_, ...), custom_call_target="tpu_custom_call" | custom-call | tf_op jit(solution)/shard_map/pallas_call | solution.py:305
  171.1 19.9 %cross.1 = bf16[64,128,128]{2,1,0:T(8,128)(2,1)} custom-call(s32[1]{0:T(128)} %bitcast.2.me, s32[4,16]{1,0:T(4,128)} %bitcast.17, s32[4,64]{1,0:T(4,128)} %place_tables.1.places, s32[1,8,128]{2,1,0:T(8,128)} %get-tuple-element.28.cls, bf16[8,128,128]{2,1,0:T(8,128)(2,1)} %recoup.13, f32[1,128,128]{2,1,0:T(8,128)} %get-tuple-element.29.down, ...), custom_call_target="tpu_custom_call" | custom-call | tf_op jit(solution)/shard_map/cross/pallas_call | solution.py:387
  191.0 13.8 %all-to-all-start.2 = ((bf16[64,128,128]{2,1,0:T(8,128)(2,1)}), bf16[64,128,128]{2,1,0:T(8,128)(2,1)S(1)}, u32[]{:S(2)}, u32[]{:S(2)}) async-start(bf16[64,128,128]{2,1,0:T(8,128)(2,1)} %cross.1), calls=%async_computation.2 | async-start | bytes 4194304 | tf_op jit(solution)/shard_map/all_to_all | solution.py:498
  204.8 3.3 %share_blocks.1 = (bf16[1280,512]{1,0:T(8,128)(2,1)}, bf16[1280,512]{1,0:T(8,128)(2,1)}) custom-call(s32[1]{0:T(128)} %bitcast.2.me, bf16[512,2048]{1,0:T(8,128)(2,1)} %bitcast.8), custom_call_target="tpu_custom_call" | custom-call | tf_op jit(solution)/shard_map/share_blocks/pallas_call | solution.py:111
  208.0 2.7 collective-permute-start.1
  210.7 28.6 %collective-permute-done.from_left = bf16[1280,512]{1,0:T(8,128)(2,1)S(1)} collective-permute-done((bf16[1280,512]{1,0:T(8,128)(2,1)}, bf16[1280,512]{1,0:T(8,128)(2,1)S(1)}, u32[]{:S(2)}, u32[]{:S(2)}) %collective-permute-start) | collective-permute-done | bytes 1310752 | tf_op jit(solution)/shard_map/ppermute | solution.py:468
  240.7 2.8 %collective-permute-start.3 = (bf16[256,512]{1,0:T(8,128)(2,1)S(1)}, bf16[256,512]{1,0:T(8,128)(2,1)S(1)}, u32[]{:S(2)}, u32[]{:S(2)}) collective-permute-start(bf16[256,512]{1,0:T(8,128)(2,1)S(1)} %slice.25), channel_id=1, source_target_pairs={{0,3},{1,0},{2,1},{3,2},{4,7},{5,4},{6,5},{7,6},{8,11},{9,8},{10,9... | collective-permute-start | bytes 786440 | tf_op jit(solution)/shard_map/ppermute | solution.py:471
  243.5 3.7 %collective-permute-done.2.far_a = bf16[256,512]{1,0:T(8,128)(2,1)S(1)} collective-permute-done((bf16[256,512]{1,0:T(8,128)(2,1)S(1)}, bf16[256,512]{1,0:T(8,128)(2,1)S(1)}, u32[]{:S(2)}, u32[]{:S(2)}) %collective-permute-start.2) | collective-permute-done | bytes 262176 | tf_op jit(solution)/shard_map/ppermute | solution.py:470
  248.7 25.5 %ladder.1.base = f32[512,2048]{1,0:T(8,128)} custom-call(s32[1]{0:T(128)} %bitcast.2.me, bf16[512,2048]{1,0:T(8,128)(2,1)} %bitcast.9, bf16[1280,512]{1,0:T(8,128)(2,1)} %copy-done.6, bf16[1280,512]{1,0:T(8,128)(2,1)} %copy-done.7, bf16[256,512]{1,0:T(8,128)(2,1)} %copy-done.10, bf16[256,512]{1,0:T(8,128)(2,1)} %copy-done.11, f32[1,2048]{1,0:T(1,128)} %energy.5, ...), custom_call_target="tpu_custom_call" | custom-call | tf_op jit(solution)/shard_map/ladder/pallas_call | solution.py:177
  275.5 5.8 %finish.1 = f32[512,2048]{1,0:T(8,128)} custom-call(s32[4,16]{1,0:T(4,128)} %bitcast.12, s32[4,16]{1,0:T(4,128)} %bitcast.15, bf16[8,128,128]{2,1,0:T(8,128)(2,1)} %recoup.13, f32[512,2048]{1,0:T(8,128)} %ladder.1.base, bf16[64,128,128]{2,1,0:T(8,128)(2,1)} %copy-done), custom_call_target="tpu_custom_call" | custom-call | tf_op jit(solution)/shard_map/finish/pallas_call | solution.py:433
  (62 shorter events, 24.0 us)
Async XLA Ops:
  3.7 43.6 %all-to-all-start = ((bf16[64,72,128]{2,1,0:T(8,128)(2,1)}), bf16[64,72,128]{2,1,0:T(8,128)(2,1)S(1)}, u32[]{:S(2)}, u32[]{:S(2)}) async-start(bf16[64,72,128]{2,1,0:T(8,128)(2,1)} %shard_map.73), calls=%async_computation | async-start | bytes 2359296 | tf_op jit(solution)/shard_map/all_to_all | solution.py:465
  47.3 41.9 %copy-start.1 = (bf16[64,72,128]{2,1,0:T(8,128)(2,1)}, bf16[64,72,128]{2,1,0:T(8,128)(2,1)S(1)}, u32[]{:S(2)}) copy-start(bf16[64,72,128]{2,1,0:T(8,128)(2,1)S(1)} %all-to-all-done.refs_0_) | copy-start | bytes 3538948
  47.3 34.8 %all-to-all-start.1 = ((bf16[64,64,128]{2,1,0:T(8,128)(2,1)}), bf16[64,64,128]{2,1,0:T(8,128)(2,1)S(1)}, u32[]{:S(2)}, u32[]{:S(2)}) async-start(bf16[64,64,128]{2,1,0:T(8,128)(2,1)} %shard_map.77), calls=%async_computation.1 | async-start | bytes 2097152 | tf_op jit(solution)/shard_map/all_to_all | solution.py:465
  53.9 57.6 %copy-start.12 = (s32[1,4,16]{2,1,0:T(4,128)S(1)}, s32[1,4,16]{2,1,0:T(4,128)}, u32[]{:S(2)}) copy-start(s32[1,4,16]{2,1,0:T(4,128)} %param.13) | copy-start | bytes 772
  53.9 30.9 %collective-permute-start.9 = (bf16[64,72,128]{2,1,0:T(8,128)(2,1)S(1)}, bf16[64,72,128]{2,1,0:T(8,128)(2,1)S(1)}, u32[]{:S(2)}, u32[]{:S(2)}) collective-permute-start(bf16[64,72,128]{2,1,0:T(8,128)(2,1)S(1)} %all-to-all-done.refs_0_), channel_id=1, source_target_pairs={{0,3},{1,0},{2,1},{3,2},{4,7},{5,4},{6,5},{7,6},{8,11},{9,8},{10,9... | collective-permute-start | bytes 3538952 | tf_op jit(solution)/shard_map/ppermute | solution.py:491
  56.7 30.5 %collective-permute-start.7 = (bf16[64,72,128]{2,1,0:T(8,128)(2,1)S(1)}, bf16[64,72,128]{2,1,0:T(8,128)(2,1)}, u32[]{:S(2)}, u32[]{:S(2)}) collective-permute-start(bf16[64,72,128]{2,1,0:T(8,128)(2,1)S(1)} %all-to-all-done.refs_0_), channel_id=1, source_target_pairs={{0,1},{1,2},{2,3},{3,0},{4,5},{5,6},{6,7},{7,4},{8,9},{9,10},{10,1... | collective-permute-start | bytes 3538952 | tf_op jit(solution)/shard_map/ppermute | solution.py:490
  82.1 26.7 %copy-start.2 = (bf16[64,64,128]{2,1,0:T(8,128)(2,1)}, bf16[64,64,128]{2,1,0:T(8,128)(2,1)S(1)}, u32[]{:S(2)}) copy-start(bf16[64,64,128]{2,1,0:T(8,128)(2,1)S(1)} %all-to-all-done.1.refs_0_) | copy-start | bytes 3145732
  82.1 24.9 %collective-permute-start.12 = (bf16[64,64,128]{2,1,0:T(8,128)(2,1)S(1)}, bf16[64,64,128]{2,1,0:T(8,128)(2,1)S(1)}, u32[]{:S(2)}, u32[]{:S(2)}) collective-permute-start(bf16[64,64,128]{2,1,0:T(8,128)(2,1)S(1)} %all-to-all-done.1.refs_0_), channel_id=1, source_target_pairs={{0,1},{1,2},{2,3},{3,0},{4,5},{5,6},{6,7},{7,4},{8,9},{9,10},{10,1... | collective-permute-start | bytes 3145736 | tf_op jit(solution)/shard_map/ppermute | solution.py:490
  83.4 24.5 %collective-permute-start.11 = (bf16[64,64,128]{2,1,0:T(8,128)(2,1)S(1)}, bf16[64,64,128]{2,1,0:T(8,128)(2,1)S(1)}, u32[]{:S(2)}, u32[]{:S(2)}) collective-permute-start(bf16[64,64,128]{2,1,0:T(8,128)(2,1)S(1)} %all-to-all-done.1.refs_0_), channel_id=1, source_target_pairs={{0,3},{1,0},{2,1},{3,2},{4,7},{5,4},{6,5},{7,6},{8,11},{9,8},{10,9... | collective-permute-start | bytes 3145736 | tf_op jit(solution)/shard_map/ppermute | solution.py:491
  84.8 24.0 %copy-start.3 = (bf16[64,72,128]{2,1,0:T(8,128)(2,1)}, bf16[64,72,128]{2,1,0:T(8,128)(2,1)S(1)}, u32[]{:S(2)}) copy-start(bf16[64,72,128]{2,1,0:T(8,128)(2,1)S(1)} %collective-permute-done.9.refs_0_) | copy-start | bytes 3538948
  85.7 79.2 %collective-permute-start.10 = (bf16[32,72,128]{2,1,0:T(8,128)(2,1)}, bf16[32,72,128]{2,1,0:T(8,128)(2,1)}, u32[]{:S(2)}, u32[]{:S(2)}) collective-permute-start(bf16[32,72,128]{2,1,0:T(8,128)(2,1)} %slice.27), channel_id=1, source_target_pairs={{0,3},{1,0},{2,1},{3,2},{4,7},{5,4},{6,5},{7,6},{8,11},{9,8},{10,9... | collective-permute-start | bytes 1769480 | tf_op jit(solution)/shard_map/ppermute | solution.py:492
  89.1 75.8 %collective-permute-start.8 = (bf16[32,72,128]{2,1,0:T(8,128)(2,1)}, bf16[32,72,128]{2,1,0:T(8,128)(2,1)}, u32[]{:S(2)}, u32[]{:S(2)}) collective-permute-start(bf16[32,72,128]{2,1,0:T(8,128)(2,1)} %slice.26), channel_id=1, source_target_pairs={{0,1},{1,2},{2,3},{3,0},{4,5},{5,6},{6,7},{7,4},{8,9},{9,10},{10,1... | collective-permute-start | bytes 1769480 | tf_op jit(solution)/shard_map/ppermute | solution.py:492
  107.9 62.2 %collective-permute-start.13 = (bf16[32,64,128]{2,1,0:T(8,128)(2,1)}, bf16[32,64,128]{2,1,0:T(8,128)(2,1)S(1)}, u32[]{:S(2)}, u32[]{:S(2)}) collective-permute-start(bf16[32,64,128]{2,1,0:T(8,128)(2,1)} %slice.28), channel_id=1, source_target_pairs={{0,1},{1,2},{2,3},{3,0},{4,5},{5,6},{6,7},{7,4},{8,9},{9,10},{10,1... | collective-permute-start | bytes 1572872 | tf_op jit(solution)/shard_map/ppermute | solution.py:492
  108.8 61.3 %collective-permute-start.14 = (bf16[32,64,128]{2,1,0:T(8,128)(2,1)}, bf16[32,64,128]{2,1,0:T(8,128)(2,1)S(1)}, u32[]{:S(2)}, u32[]{:S(2)}) collective-permute-start(bf16[32,64,128]{2,1,0:T(8,128)(2,1)} %slice.29), channel_id=1, source_target_pairs={{0,3},{1,0},{2,1},{3,2},{4,7},{5,4},{6,5},{7,6},{8,11},{9,8},{10,9... | collective-permute-start | bytes 1572872 | tf_op jit(solution)/shard_map/ppermute | solution.py:492
  111.5 19.4 %collective-permute-start.6 = (s32[4,16]{1,0:T(4,128)S(1)}, s32[4,16]{1,0:T(4,128)S(1)}, u32[]{:S(2)}, u32[]{:S(2)}) collective-permute-start(s32[4,16]{1,0:T(4,128)S(1)} %bitcast.18), channel_id=1, source_target_pairs={{0,1},{1,2},{2,3},{3,0},{4,5},{5,6},{6,7},{7,4},{8,9},{9,10},{10,1... | collective-permute-start | bytes 776 | tf_op jit(solution)/shard_map/ppermute | solution.py:476
  130.9 6.6 %copy-start.13 = (s32[4,16]{1,0:T(4,128)}, s32[4,16]{1,0:T(4,128)S(1)}, u32[]{:S(2)}) copy-start(s32[4,16]{1,0:T(4,128)S(1)} %collective-permute-done.6.left) | copy-start | bytes 772
  130.9 3.9 %collective-permute-start.5 = (s32[4,16]{1,0:T(4,128)S(1)}, s32[4,16]{1,0:T(4,128)S(1)}, u32[]{:S(2)}, u32[]{:S(2)}) collective-permute-start(s32[4,16]{1,0:T(4,128)S(1)} %bitcast.19), channel_id=1, source_target_pairs={{0,2},{1,3},{2,0},{3,1},{4,6},{5,7},{6,4},{7,5},{8,10},{9,11},{10,... | collective-permute-start | bytes 776 | tf_op jit(solution)/shard_map/ppermute | solution.py:475
  134.8 2.7 collective-permute-start.4
  191.0 83.1 %all-to-all-start.2 = ((bf16[64,128,128]{2,1,0:T(8,128)(2,1)}), bf16[64,128,128]{2,1,0:T(8,128)(2,1)S(1)}, u32[]{:S(2)}, u32[]{:S(2)}) async-start(bf16[64,128,128]{2,1,0:T(8,128)(2,1)} %cross.1), calls=%async_computation.2 | async-start | bytes 4194304 | tf_op jit(solution)/shard_map/all_to_all | solution.py:498
  208.0 31.3 %collective-permute-start = (bf16[1280,512]{1,0:T(8,128)(2,1)}, bf16[1280,512]{1,0:T(8,128)(2,1)S(1)}, u32[]{:S(2)}, u32[]{:S(2)}) collective-permute-start(bf16[1280,512]{1,0:T(8,128)(2,1)} %get-tuple-element.26), channel_id=1, source_target_pairs={{0,1},{1,2},{2,3},{3,0},{4,5},{5,6},{6,7},{7,4},{8,9},{9,10},{10,1... | collective-permute-start | bytes 3932168 | tf_op jit(solution)/shard_map/ppermute | solution.py:468
  208.0 31.4 %collective-permute-start.1 = (bf16[1280,512]{1,0:T(8,128)(2,1)}, bf16[1280,512]{1,0:T(8,128)(2,1)S(1)}, u32[]{:S(2)}, u32[]{:S(2)}) collective-permute-start(bf16[1280,512]{1,0:T(8,128)(2,1)} %get-tuple-element.27), channel_id=1, source_target_pairs={{0,3},{1,0},{2,1},{3,2},{4,7},{5,4},{6,5},{7,6},{8,11},{9,8},{10,9... | collective-permute-start | bytes 3932168 | tf_op jit(solution)/shard_map/ppermute | solution.py:469
  239.3 8.2 %copy-start.6 = (bf16[1280,512]{1,0:T(8,128)(2,1)}, bf16[1280,512]{1,0:T(8,128)(2,1)S(1)}, u32[]{:S(2)}) copy-start(bf16[1280,512]{1,0:T(8,128)(2,1)S(1)} %collective-permute-done.from_left) | copy-start | bytes 3932164
  239.4 7.8 %collective-permute-start.2 = (bf16[256,512]{1,0:T(8,128)(2,1)S(1)}, bf16[256,512]{1,0:T(8,128)(2,1)S(1)}, u32[]{:S(2)}, u32[]{:S(2)}) collective-permute-start(bf16[256,512]{1,0:T(8,128)(2,1)S(1)} %slice.24), channel_id=1, source_target_pairs={{0,1},{1,2},{2,3},{3,0},{4,5},{5,6},{6,7},{7,4},{8,9},{9,10},{10,1... | collective-permute-start | bytes 786440 | tf_op jit(solution)/shard_map/ppermute | solution.py:470
  240.7 6.9 %collective-permute-start.3 = (bf16[256,512]{1,0:T(8,128)(2,1)S(1)}, bf16[256,512]{1,0:T(8,128)(2,1)S(1)}, u32[]{:S(2)}, u32[]{:S(2)}) collective-permute-start(bf16[256,512]{1,0:T(8,128)(2,1)S(1)} %slice.25), channel_id=1, source_target_pairs={{0,3},{1,0},{2,1},{3,2},{4,7},{5,4},{6,5},{7,6},{8,11},{9,8},{10,9... | collective-permute-start | bytes 786440 | tf_op jit(solution)/shard_map/ppermute | solution.py:471
  (10 other events, 17.2 us)

commit v3 on v2

--- a/solution.py
+++ b/solution.py
@@ -321,14 +321,14 @@
     rows_down = recv.shape[0]
     width = pieces[0].shape[2]
     late = body_copies(raws, raw, sems)
-    copies = []
+    eta_copies, gamma_copies = [[] for _ in range(4)], []
     for n, (part, block, key, place) in enumerate(blocks):
         where = pl.ds(((me[0] + block) % 4) * rows_down, rows_down)
-        for which, target in enumerate((eta, gamma)):
+        for which, (target, group) in enumerate(((eta, eta_copies[block]), (gamma, gamma_copies))):
             source = pieces[2 * key + which].at[pl.ds(place * rows_down, rows_down)]
             into = target.at[where, pl.ds(part * ROWS, ROWS), :]
-            copies.append(pltpu.make_async_copy(source, into, piece_sems.at[2 * n + which]))
-    for copy in late + copies:
+            group.append(pltpu.make_async_copy(source, into, piece_sems.at[2 * n + which]))
+    for copy in late + gamma_copies + [copy for group in eta_copies for copy in group]:
         copy.start()
     for copy in late:
         copy.wait()
@@ -342,18 +342,26 @@
     recouple_block(
         chunk, width // TB, raw, down.at[0], along.at[0], lambda q: cls[0, 0, count + q], places, 2, recoup, put
     )
-    for copy in copies:
+    for copy in gamma_copies + eta_copies[0]:
         copy.wait()
     side = rows_down * TB
     mine = pl.ds(me[0] * rows_down, rows_down)
     for i in range(rows_down):
         cols = pl.ds(pl.multiple_of((me[0] * rows_down + i) * TB, TB), TB)
         for k in range(4 * rows_down):
-            tile = gamma[k, :, cols].astype(F32)
-            turned[i * TB : (i + 1) * TB, k * TB : (k + 1) * TB] = jnp.transpose(tile).astype(BF)
+            turned[i * TB : (i + 1) * TB, k * TB : (k + 1) * TB] = jnp.transpose(gamma[k, :, cols])
     step = 2
-
-    def body(n, carry):
+    turns = rows_down // step
+
+    def body(t, carry):
+        for block in range(1, 4):
+
+            @pl.when(t == block * turns)
+            def _(block=block):
+                for copy in eta_copies[block]:
+                    copy.wait()
+
+        n = ((me[0] + t // turns) % 4) * turns + t % turns
         cols = pl.ds(pl.multiple_of(n * step * TB, step * TB), step * TB)
         half = jnp.dot(
             eta[mine].reshape(side, width),
@@ -372,7 +380,7 @@
                 out[recv[i, n * step + j]] = result[i * TB : (i + 1) * TB, j * TB : (j + 1) * TB]
         return carry
 
-    lax.fori_loop(0, width // (step * TB), body, 0)
+    lax.fori_loop(0, 4 * turns, body, 0)
 
 
 def cross(chunk, me, recv, places, recoup, pieces, raws, codes):
@@ -402,10 +410,8 @@
     )(me, recv, places, cls, recoup, down, along, *flat, *raws)
 
 
-def final_kernel(step_size, send, cls, recoup, base, back, out, total, tiles, sems, out_sems):
+def final_kernel(step_size, send, cls, recoup, tiles, base, out, total, sems, out_sems):
     rows_down, across = send.shape
-    arrive = pltpu.make_async_copy(back, tiles, sems.at[rows_down])
-    arrive.start()
     copies, leaves = [], []
     for i in range(rows_down):
         rows = pl.ds(i * TB, TB)
@@ -413,7 +419,6 @@
         leaves.append(pltpu.make_async_copy(total.at[rows], out.at[rows], out_sems.at[i]))
     for copy in copies:
         copy.start()
-    arrive.wait()
     for i in range(rows_down):
         copies[i].wait()
         rows = slice(i * TB, (i + 1) * TB)
@@ -433,17 +438,16 @@
     return pl.pallas_call(
         functools.partial(final_kernel, step_size),
         out_shape=jax.ShapeDtypeStruct(base.shape, F32),
-        in_specs=[SMEM, SMEM, VMEM, ANY, ANY],
+        in_specs=[SMEM, SMEM, VMEM, VMEM, ANY],
         out_specs=ANY,
         scratch_shapes=[
             pltpu.VMEM(base.shape, F32),
-            pltpu.VMEM(back.shape, BF),
-            pltpu.SemaphoreType.DMA((rows_down + 1,)),
+            pltpu.SemaphoreType.DMA((rows_down,)),
             pltpu.SemaphoreType.DMA((rows_down,)),
         ],
         compiler_params=BIG,
         name="finish",
-    )(send, cls, recoup, base, back)
+    )(send, cls, recoup, pltpu.with_memory_space_constraint(back, pltpu.VMEM), base)
 
 
 RIGHT = [(i, (i + 1) % 4) for i in range(4)]

time: 284 us -> 281 us (0.989)
  no operation moved by 1% of the time
where the time goes in v3:
time: 281 us; the launch traced here: 279 us
  waiting for transfers between devices  126 us (45%)
  Pallas kernels  92.6 us (33%)
  starting transfers between devices  51.7 us (18%)
  local copies, waits for them, and re-layouts  8.5 us (3%)
    all_to_all x2, waiting for transfers between devices, on_device(): lax.all_to_all(buf, 'chan', split_axis=0, concat_axis=0, tiled=True)  52.5 us
    ppermute x1, waiting for transfers between devices, on_device(): from_left = lax.ppermute(to_right, 'tile', RIGHT)  28.6 us
    pallas_call x5, Pallas kernels, recouple(): pl.pallas_call(functools.partial(recouple_kernel, chunk, across, parts, b...  28.2 us
    pallas_call x1, Pallas kernels, ladder_base(): pl.pallas_call(functools.partial(ladder_kernel, step_size), out_shape=jax...  25.5 us
    pallas_call x1, Pallas kernels, cross(): pl.pallas_call(functools.partial(cross_kernel, chunk, blocks, len(raws)),...  19.6 us
    all_to_all x2, starting transfers between devices, on_device(): lax.all_to_all(buf, 'chan', split_axis=0, concat_axis=0, tiled=True)  19.6 us
    ppermute x1, waiting for transfers between devices, on_device(): lax.ppermute(recv, 'tile', RIGHT)  19.3 us
    ppermute x2, waiting for transfers between devices, on_device(): left = lax.ppermute(own, 'tile', RIGHT)  17.8 us
  transfers between devices with their start and end apart: 18, of which 9 were waited for; matrix products, arithmetic and copies ran while one was open for 2% of the time, Pallas kernels for 23%

profile of v3, /device:TPU:1, one launch (start us, length us, event | category | flops | bytes accessed | tf_op | source)
XLA Modules:
  0.0 279.2 jit_solution(9930206536366954052)
XLA Ops:
  0.0 3.7 %shard_map.73 = bf16[64,72,128]{2,1,0:T(8,128)(2,1)} custom-call(s32[1]{0:T(128)} %bitcast.2.me, s32[4,16]{1,0:T(4,128)} %bitcast.10, s32[4,16]{1,0:T(4,128)} %bitcast.13, bf16[512,2048]{1,0:T(8,128)(2,1)} %bitcast.6, f32[1,2048]{1,0:T(1,128)} %energy.5, s32[1,2048]{1,0:T(1,128)} %occ.5), custom_call_target="tpu_custom_call" | custom-call | tf_op jit(solution)/shard_map/pallas_call | solution.py:60
  3.7 13.0 %all-to-all-start = ((bf16[64,72,128]{2,1,0:T(8,128)(2,1)}), bf16[64,72,128]{2,1,0:T(8,128)(2,1)S(1)}, u32[]{:S(2)}, u32[]{:S(2)}) async-start(bf16[64,72,128]{2,1,0:T(8,128)(2,1)} %shard_map.73), calls=%async_computation | async-start | bytes 2359296 | tf_op jit(solution)/shard_map/all_to_all | solution.py:469
  16.7 3.5 %shard_map.77 = bf16[64,64,128]{2,1,0:T(8,128)(2,1)} custom-call(s32[1]{0:T(128)} %bitcast.2.me, s32[4,16]{1,0:T(4,128)} %bitcast.11, s32[4,16]{1,0:T(4,128)} %bitcast.14, bf16[512,2048]{1,0:T(8,128)(2,1)} %bitcast.7, f32[1,2048]{1,0:T(1,128)} %energy.5, s32[1,2048]{1,0:T(1,128)} %occ.5), custom_call_target="tpu_custom_call" | custom-call | tf_op jit(solution)/shard_map/pallas_call | solution.py:60
  20.1 27.1 %all-to-all-done.refs_0_ = bf16[64,72,128]{2,1,0:T(8,128)(2,1)S(1)} async-done(((bf16[64,72,128]{2,1,0:T(8,128)(2,1)}), bf16[64,72,128]{2,1,0:T(8,128)(2,1)S(1)}, u32[]{:S(2)}, u32[]{:S(2)}) %all-to-all-start) | async-done | bytes 1179680 | tf_op jit(solution)/shard_map/all_to_all | solution.py:469
  47.3 6.6 %all-to-all-start.1 = ((bf16[64,64,128]{2,1,0:T(8,128)(2,1)}), bf16[64,64,128]{2,1,0:T(8,128)(2,1)S(1)}, u32[]{:S(2)}, u32[]{:S(2)}) async-start(bf16[64,64,128]{2,1,0:T(8,128)(2,1)} %shard_map.77), calls=%async_computation.1 | async-start | bytes 2097152 | tf_op jit(solution)/shard_map/all_to_all | solution.py:469
  53.9 2.8 %collective-permute-start.5 = (bf16[64,72,128]{2,1,0:T(8,128)(2,1)S(1)}, bf16[64,72,128]{2,1,0:T(8,128)(2,1)S(1)}, u32[]{:S(2)}, u32[]{:S(2)}) collective-permute-start(bf16[64,72,128]{2,1,0:T(8,128)(2,1)S(1)} %all-to-all-done.refs_0_), channel_id=1, source_target_pairs={{0,3},{1,0},{2,1},{3,2},{4,7},{5,4},{6,5},{7,6},{8,11},{9,8},{10,9... | collective-permute-start | bytes 3538952 | tf_op jit(solution)/shard_map/ppermute | solution.py:495
  56.7 25.3 %all-to-all-done.1.refs_0_ = bf16[64,64,128]{2,1,0:T(8,128)(2,1)S(1)} async-done(((bf16[64,64,128]{2,1,0:T(8,128)(2,1)}), bf16[64,64,128]{2,1,0:T(8,128)(2,1)S(1)}, u32[]{:S(2)}, u32[]{:S(2)}) %all-to-all-start.1) | async-done | bytes 1048608 | tf_op jit(solution)/shard_map/all_to_all | solution.py:469
  89.1 17.8 %collective-permute-done.8.refs_1_ = bf16[64,64,128]{2,1,0:T(8,128)(2,1)S(1)} collective-permute-done((bf16[64,64,128]{2,1,0:T(8,128)(2,1)S(1)}, bf16[64,64,128]{2,1,0:T(8,128)(2,1)S(1)}, u32[]{:S(2)}, u32[]{:S(2)}) %collective-permute-start.8) | collective-permute-done | bytes 1048608 | tf_op jit(solution)/shard_map/ppermute | solution.py:494
  111.6 19.3 %collective-permute-done.2.left = s32[4,16]{1,0:T(4,128)S(1)} collective-permute-done((s32[4,16]{1,0:T(4,128)S(1)}, s32[4,16]{1,0:T(4,128)S(1)}, u32[]{:S(2)}, u32[]{:S(2)}) %collective-permute-start.2) | collective-permute-done | bytes 288 | tf_op jit(solution)/shard_map/ppermute | solution.py:480
  138.1 3.7 %place_tables.1.places = s32[4,64]{1,0:T(4,128)} custom-call(s32[4,16]{1,0:T(4,128)} %bitcast.16, s32[4,16]{1,0:T(4,128)} %copy-done.14, s32[4,16]{1,0:T(4,128)} %copy-done.13, s32[4,16]{1,0:T(4,128)} %copy-done.12), custom_call_target="tpu_custom_call" | custom-call | tf_op jit(solution)/shard_map/place_tables/pallas_call | solution.py:81
  141.8 5.0 %shard_map.75 = (bf16[4,64,2048]{2,1,0:T(8,128)(2,1)}, bf16[4,64,2048]{2,1,0:T(8,128)(2,1)}, f32[1,128,128]{2,1,0:T(8,128)}, f32[1,64,128]{2,1,0:T(8,128)}, s32[1,8,128]{2,1,0:T(8,128)}) custom-call(s32[4,64]{1,0:T(4,128)} %place_tables.1.places, bf16[8,128,128]{2,1,0:T(8,128)(2,1)} %recoup.13, bf16[64,72,128]{2,1,0:T(8,128)(2,1)} %copy-done), custom_call_target="tpu_custom_call" | custom-call | tf_op jit(solution)/shard_map/pallas_call | solution.py:305
  146.7 4.5 %shard_map.78 = (bf16[4,64,2048]{2,1,0:T(8,128)(2,1)}, bf16[4,64,2048]{2,1,0:T(8,128)(2,1)}) custom-call(s32[4,64]{1,0:T(4,128)} %place_tables.1.places, bf16[8,128,128]{2,1,0:T(8,128)(2,1)} %recoup.13, bf16[64,64,128]{2,1,0:T(8,128)(2,1)} %copy-done.1, f32[1,128,128]{2,1,0:T(8,128)} %get-tuple-element.35.refs_1_, f32[1,64,128]{2,1,0:T(8,128)} %get-tuple-element.36.refs_2_, ...), custom_call_target="tpu_custom_call" | custom-call | tf_op jit(solution)/shard_map/pallas_call | solution.py:305
  151.2 7.4 %shard_map.76 = (bf16[8,64,2048]{2,1,0:T(8,128)(2,1)}, bf16[8,64,2048]{2,1,0:T(8,128)(2,1)}, f32[2,128,128]{2,1,0:T(8,128)}, f32[2,64,128]{2,1,0:T(8,128)}, s32[2,8,128]{2,1,0:T(8,128)}) custom-call(s32[4,64]{1,0:T(4,128)} %place_tables.1.places, bf16[8,128,128]{2,1,0:T(8,128)(2,1)} %recoup.13, bf16[64,72,128]{2,1,0:T(8,128)(2,1)} %copy-done.2, ...), custom_call_target="tpu_custom_call" | custom-call | tf_op jit(solution)/shard_map/pallas_call | solution.py:305
  158.6 6.3 %shard_map.79 = (bf16[8,64,2048]{2,1,0:T(8,128)(2,1)}, bf16[8,64,2048]{2,1,0:T(8,128)(2,1)}) custom-call(s32[4,64]{1,0:T(4,128)} %place_tables.1.places, bf16[8,128,128]{2,1,0:T(8,128)(2,1)} %recoup.13, bf16[64,64,128]{2,1,0:T(8,128)(2,1)} %copy-done.4, bf16[64,64,128]{2,1,0:T(8,128)(2,1)} %copy-done.3, f32[2,128,128]{2,1,0:T(8,128)} %get-tuple-element.40.refs_2_, ...), custom_call_target="tpu_custom_call" | custom-call | tf_op jit(solution)/shard_map/pallas_call | solution.py:305
  165.0 5.1 %shard_map.74 = (bf16[4,64,2048]{2,1,0:T(8,128)(2,1)}, bf16[4,64,2048]{2,1,0:T(8,128)(2,1)}, f32[1,128,128]{2,1,0:T(8,128)}, f32[1,64,128]{2,1,0:T(8,128)}, s32[1,8,128]{2,1,0:T(8,128)}) custom-call(s32[4,64]{1,0:T(4,128)} %place_tables.1.places, bf16[8,128,128]{2,1,0:T(8,128)(2,1)} %recoup.13, bf16[32,72,128]{2,1,0:T(8,128)(2,1)} %collective-permute-done.4.refs_0_, ...), custom_call_target="tpu_custom_call" | custom-call | tf_op jit(solution)/shard_map/pallas_call | solution.py:305
  171.0 19.6 %cross.1 = bf16[64,128,128]{2,1,0:T(8,128)(2,1)} custom-call(s32[1]{0:T(128)} %bitcast.2.me, s32[4,16]{1,0:T(4,128)} %bitcast.17, s32[4,64]{1,0:T(4,128)} %place_tables.1.places, s32[1,8,128]{2,1,0:T(8,128)} %get-tuple-element.26.cls, bf16[8,128,128]{2,1,0:T(8,128)(2,1)} %recoup.13, f32[1,128,128]{2,1,0:T(8,128)} %get-tuple-element.27.down, ...), custom_call_target="tpu_custom_call" | custom-call | tf_op jit(solution)/shard_map/cross/pallas_call | solution.py:395
  190.7 13.8 %all-to-all-start.2 = ((bf16[64,128,128]{2,1,0:T(8,128)(2,1)}), bf16[64,128,128]{2,1,0:T(8,128)(2,1)S(1)}, u32[]{:S(2)}, u32[]{:S(2)}) async-start(bf16[64,128,128]{2,1,0:T(8,128)(2,1)} %cross.1), calls=%async_computation.2 | async-start | bytes 4194304 | tf_op jit(solution)/shard_map/all_to_all | solution.py:502
  204.5 3.3 %share_blocks.1 = (bf16[1280,512]{1,0:T(8,128)(2,1)}, bf16[1280,512]{1,0:T(8,128)(2,1)}) custom-call(s32[1]{0:T(128)} %bitcast.2.me, bf16[512,2048]{1,0:T(8,128)(2,1)} %bitcast.8), custom_call_target="tpu_custom_call" | custom-call | tf_op jit(solution)/shard_map/share_blocks/pallas_call | solution.py:111
  207.7 2.7 collective-permute-start.12
  210.4 28.6 %collective-permute-done.11.from_left = bf16[1280,512]{1,0:T(8,128)(2,1)S(1)} collective-permute-done((bf16[1280,512]{1,0:T(8,128)(2,1)}, bf16[1280,512]{1,0:T(8,128)(2,1)S(1)}, u32[]{:S(2)}, u32[]{:S(2)}) %collective-permute-start.11) | collective-permute-done | bytes 1310752 | tf_op jit(solution)/shard_map/ppermute | solution.py:472
  240.3 2.9 %collective-permute-start.14 = (bf16[256,512]{1,0:T(8,128)(2,1)S(1)}, bf16[256,512]{1,0:T(8,128)(2,1)S(1)}, u32[]{:S(2)}, u32[]{:S(2)}) collective-permute-start(bf16[256,512]{1,0:T(8,128)(2,1)S(1)} %slice.29), channel_id=1, source_target_pairs={{0,3},{1,0},{2,1},{3,2},{4,7},{5,4},{6,5},{7,6},{8,11},{9,8},{10,9... | collective-permute-start | bytes 786440 | tf_op jit(solution)/shard_map/ppermute | solution.py:475
  243.2 3.7 %collective-permute-done.13.far_a = bf16[256,512]{1,0:T(8,128)(2,1)S(1)} collective-permute-done((bf16[256,512]{1,0:T(8,128)(2,1)S(1)}, bf16[256,512]{1,0:T(8,128)(2,1)S(1)}, u32[]{:S(2)}, u32[]{:S(2)}) %collective-permute-start.13) | collective-permute-done | bytes 262176 | tf_op jit(solution)/shard_map/ppermute | solution.py:474
  248.4 25.5 %ladder.1.base = f32[512,2048]{1,0:T(8,128)} custom-call(s32[1]{0:T(128)} %bitcast.2.me, bf16[512,2048]{1,0:T(8,128)(2,1)} %bitcast.9, bf16[1280,512]{1,0:T(8,128)(2,1)} %copy-done.5, bf16[1280,512]{1,0:T(8,128)(2,1)} %copy-done.6, bf16[256,512]{1,0:T(8,128)(2,1)} %copy-done.9, bf16[256,512]{1,0:T(8,128)(2,1)} %copy-done.10, f32[1,2048]{1,0:T(1,128)} %energy.5, ...), custom_call_target="tpu_custom_call" | custom-call | tf_op jit(solution)/shard_map/ladder/pallas_call | solution.py:177
  273.9 5.1 %finish.1 = f32[512,2048]{1,0:T(8,128)} custom-call(s32[4,16]{1,0:T(4,128)} %bitcast.12, s32[4,16]{1,0:T(4,128)} %bitcast.15, bf16[8,128,128]{2,1,0:T(8,128)(2,1)} %recoup.13, bf16[64,128,128]{2,1,0:T(8,128)(2,1)S(1)} %all-to-all-done.2.tiles, f32[512,2048]{1,0:T(8,128)} %ladder.1.base), custom_call_target="tpu_custom_call" | custom-call | tf_op jit(solution)/shard_map/finish/pallas_call | solution.py:438
  (60 shorter events, 22.6 us)
Async XLA Ops:
  3.7 43.6 %all-to-all-start = ((bf16[64,72,128]{2,1,0:T(8,128)(2,1)}), bf16[64,72,128]{2,1,0:T(8,128)(2,1)S(1)}, u32[]{:S(2)}, u32[]{:S(2)}) async-start(bf16[64,72,128]{2,1,0:T(8,128)(2,1)} %shard_map.73), calls=%async_computation | async-start | bytes 2359296 | tf_op jit(solution)/shard_map/all_to_all | solution.py:469
  47.3 41.9 %copy-start = (bf16[64,72,128]{2,1,0:T(8,128)(2,1)}, bf16[64,72,128]{2,1,0:T(8,128)(2,1)S(1)}, u32[]{:S(2)}) copy-start(bf16[64,72,128]{2,1,0:T(8,128)(2,1)S(1)} %all-to-all-done.refs_0_) | copy-start | bytes 3538948
  47.3 34.8 %all-to-all-start.1 = ((bf16[64,64,128]{2,1,0:T(8,128)(2,1)}), bf16[64,64,128]{2,1,0:T(8,128)(2,1)S(1)}, u32[]{:S(2)}, u32[]{:S(2)}) async-start(bf16[64,64,128]{2,1,0:T(8,128)(2,1)} %shard_map.77), calls=%async_computation.1 | async-start | bytes 2097152 | tf_op jit(solution)/shard_map/all_to_all | solution.py:469
  53.9 57.6 %copy-start.11 = (s32[1,4,16]{2,1,0:T(4,128)S(1)}, s32[1,4,16]{2,1,0:T(4,128)}, u32[]{:S(2)}) copy-start(s32[1,4,16]{2,1,0:T(4,128)} %param.13) | copy-start | bytes 772
  53.9 30.9 %collective-permute-start.5 = (bf16[64,72,128]{2,1,0:T(8,128)(2,1)S(1)}, bf16[64,72,128]{2,1,0:T(8,128)(2,1)S(1)}, u32[]{:S(2)}, u32[]{:S(2)}) collective-permute-start(bf16[64,72,128]{2,1,0:T(8,128)(2,1)S(1)} %all-to-all-done.refs_0_), channel_id=1, source_target_pairs={{0,3},{1,0},{2,1},{3,2},{4,7},{5,4},{6,5},{7,6},{8,11},{9,8},{10,9... | collective-permute-start | bytes 3538952 | tf_op jit(solution)/shard_map/ppermute | solution.py:495
  56.7 30.5 %collective-permute-start.3 = (bf16[64,72,128]{2,1,0:T(8,128)(2,1)S(1)}, bf16[64,72,128]{2,1,0:T(8,128)(2,1)}, u32[]{:S(2)}, u32[]{:S(2)}) collective-permute-start(bf16[64,72,128]{2,1,0:T(8,128)(2,1)S(1)} %all-to-all-done.refs_0_), channel_id=1, source_target_pairs={{0,1},{1,2},{2,3},{3,0},{4,5},{5,6},{6,7},{7,4},{8,9},{9,10},{10,1... | collective-permute-start | bytes 3538952 | tf_op jit(solution)/shard_map/ppermute | solution.py:494
  82.1 26.7 %copy-start.1 = (bf16[64,64,128]{2,1,0:T(8,128)(2,1)}, bf16[64,64,128]{2,1,0:T(8,128)(2,1)S(1)}, u32[]{:S(2)}) copy-start(bf16[64,64,128]{2,1,0:T(8,128)(2,1)S(1)} %all-to-all-done.1.refs_0_) | copy-start | bytes 3145732
  82.1 24.9 %collective-permute-start.8 = (bf16[64,64,128]{2,1,0:T(8,128)(2,1)S(1)}, bf16[64,64,128]{2,1,0:T(8,128)(2,1)S(1)}, u32[]{:S(2)}, u32[]{:S(2)}) collective-permute-start(bf16[64,64,128]{2,1,0:T(8,128)(2,1)S(1)} %all-to-all-done.1.refs_0_), channel_id=1, source_target_pairs={{0,1},{1,2},{2,3},{3,0},{4,5},{5,6},{6,7},{7,4},{8,9},{9,10},{10,1... | collective-permute-start | bytes 3145736 | tf_op jit(solution)/shard_map/ppermute | solution.py:494
  83.4 24.5 %collective-permute-start.7 = (bf16[64,64,128]{2,1,0:T(8,128)(2,1)S(1)}, bf16[64,64,128]{2,1,0:T(8,128)(2,1)S(1)}, u32[]{:S(2)}, u32[]{:S(2)}) collective-permute-start(bf16[64,64,128]{2,1,0:T(8,128)(2,1)S(1)} %all-to-all-done.1.refs_0_), channel_id=1, source_target_pairs={{0,3},{1,0},{2,1},{3,2},{4,7},{5,4},{6,5},{7,6},{8,11},{9,8},{10,9... | collective-permute-start | bytes 3145736 | tf_op jit(solution)/shard_map/ppermute | solution.py:495
  84.8 24.0 %copy-start.2 = (bf16[64,72,128]{2,1,0:T(8,128)(2,1)}, bf16[64,72,128]{2,1,0:T(8,128)(2,1)S(1)}, u32[]{:S(2)}) copy-start(bf16[64,72,128]{2,1,0:T(8,128)(2,1)S(1)} %collective-permute-done.5.refs_0_) | copy-start | bytes 3538948
  85.7 79.2 %collective-permute-start.6 = (bf16[32,72,128]{2,1,0:T(8,128)(2,1)}, bf16[32,72,128]{2,1,0:T(8,128)(2,1)}, u32[]{:S(2)}, u32[]{:S(2)}) collective-permute-start(bf16[32,72,128]{2,1,0:T(8,128)(2,1)} %slice.25), channel_id=1, source_target_pairs={{0,3},{1,0},{2,1},{3,2},{4,7},{5,4},{6,5},{7,6},{8,11},{9,8},{10,9... | collective-permute-start | bytes 1769480 | tf_op jit(solution)/shard_map/ppermute | solution.py:496
  89.1 75.8 %collective-permute-start.4 = (bf16[32,72,128]{2,1,0:T(8,128)(2,1)}, bf16[32,72,128]{2,1,0:T(8,128)(2,1)}, u32[]{:S(2)}, u32[]{:S(2)}) collective-permute-start(bf16[32,72,128]{2,1,0:T(8,128)(2,1)} %slice.24), channel_id=1, source_target_pairs={{0,1},{1,2},{2,3},{3,0},{4,5},{5,6},{6,7},{7,4},{8,9},{9,10},{10,1... | collective-permute-start | bytes 1769480 | tf_op jit(solution)/shard_map/ppermute | solution.py:496
  107.9 62.2 %collective-permute-start.9 = (bf16[32,64,128]{2,1,0:T(8,128)(2,1)}, bf16[32,64,128]{2,1,0:T(8,128)(2,1)S(1)}, u32[]{:S(2)}, u32[]{:S(2)}) collective-permute-start(bf16[32,64,128]{2,1,0:T(8,128)(2,1)} %slice.26), channel_id=1, source_target_pairs={{0,1},{1,2},{2,3},{3,0},{4,5},{5,6},{6,7},{7,4},{8,9},{9,10},{10,1... | collective-permute-start | bytes 1572872 | tf_op jit(solution)/shard_map/ppermute | solution.py:496
  108.8 61.3 %collective-permute-start.10 = (bf16[32,64,128]{2,1,0:T(8,128)(2,1)}, bf16[32,64,128]{2,1,0:T(8,128)(2,1)S(1)}, u32[]{:S(2)}, u32[]{:S(2)}) collective-permute-start(bf16[32,64,128]{2,1,0:T(8,128)(2,1)} %slice.27), channel_id=1, source_target_pairs={{0,3},{1,0},{2,1},{3,2},{4,7},{5,4},{6,5},{7,6},{8,11},{9,8},{10,9... | collective-permute-start | bytes 1572872 | tf_op jit(solution)/shard_map/ppermute | solution.py:496
  111.5 19.4 %collective-permute-start.2 = (s32[4,16]{1,0:T(4,128)S(1)}, s32[4,16]{1,0:T(4,128)S(1)}, u32[]{:S(2)}, u32[]{:S(2)}) collective-permute-start(s32[4,16]{1,0:T(4,128)S(1)} %bitcast.18), channel_id=1, source_target_pairs={{0,1},{1,2},{2,3},{3,0},{4,5},{5,6},{6,7},{7,4},{8,9},{9,10},{10,1... | collective-permute-start | bytes 776 | tf_op jit(solution)/shard_map/ppermute | solution.py:480
  130.9 6.6 %copy-start.12 = (s32[4,16]{1,0:T(4,128)}, s32[4,16]{1,0:T(4,128)S(1)}, u32[]{:S(2)}) copy-start(s32[4,16]{1,0:T(4,128)S(1)} %collective-permute-done.2.left) | copy-start | bytes 772
  130.9 3.9 %collective-permute-start.1 = (s32[4,16]{1,0:T(4,128)S(1)}, s32[4,16]{1,0:T(4,128)S(1)}, u32[]{:S(2)}, u32[]{:S(2)}) collective-permute-start(s32[4,16]{1,0:T(4,128)S(1)} %bitcast.19), channel_id=1, source_target_pairs={{0,2},{1,3},{2,0},{3,1},{4,6},{5,7},{6,4},{7,5},{8,10},{9,11},{10,... | collective-permute-start | bytes 776 | tf_op jit(solution)/shard_map/ppermute | solution.py:479
  134.8 2.7 collective-permute-start
  190.7 83.2 %all-to-all-start.2 = ((bf16[64,128,128]{2,1,0:T(8,128)(2,1)}), bf16[64,128,128]{2,1,0:T(8,128)(2,1)S(1)}, u32[]{:S(2)}, u32[]{:S(2)}) async-start(bf16[64,128,128]{2,1,0:T(8,128)(2,1)} %cross.1), calls=%async_computation.2 | async-start | bytes 4194304 | tf_op jit(solution)/shard_map/all_to_all | solution.py:502
  207.7 31.3 %collective-permute-start.11 = (bf16[1280,512]{1,0:T(8,128)(2,1)}, bf16[1280,512]{1,0:T(8,128)(2,1)S(1)}, u32[]{:S(2)}, u32[]{:S(2)}) collective-permute-start(bf16[1280,512]{1,0:T(8,128)(2,1)} %get-tuple-element.45), channel_id=1, source_target_pairs={{0,1},{1,2},{2,3},{3,0},{4,5},{5,6},{6,7},{7,4},{8,9},{9,10},{10,1... | collective-permute-start | bytes 3932168 | tf_op jit(solution)/shard_map/ppermute | solution.py:472
  207.7 31.4 %collective-permute-start.12 = (bf16[1280,512]{1,0:T(8,128)(2,1)}, bf16[1280,512]{1,0:T(8,128)(2,1)S(1)}, u32[]{:S(2)}, u32[]{:S(2)}) collective-permute-start(bf16[1280,512]{1,0:T(8,128)(2,1)} %get-tuple-element.46), channel_id=1, source_target_pairs={{0,3},{1,0},{2,1},{3,2},{4,7},{5,4},{6,5},{7,6},{8,11},{9,8},{10,9... | collective-permute-start | bytes 3932168 | tf_op jit(solution)/shard_map/ppermute | solution.py:473
  239.0 8.3 %copy-start.5 = (bf16[1280,512]{1,0:T(8,128)(2,1)}, bf16[1280,512]{1,0:T(8,128)(2,1)S(1)}, u32[]{:S(2)}) copy-start(bf16[1280,512]{1,0:T(8,128)(2,1)S(1)} %collective-permute-done.11.from_left) | copy-start | bytes 3932164
  239.0 7.8 %collective-permute-start.13 = (bf16[256,512]{1,0:T(8,128)(2,1)S(1)}, bf16[256,512]{1,0:T(8,128)(2,1)S(1)}, u32[]{:S(2)}, u32[]{:S(2)}) collective-permute-start(bf16[256,512]{1,0:T(8,128)(2,1)S(1)} %slice.28), channel_id=1, source_target_pairs={{0,1},{1,2},{2,3},{3,0},{4,5},{5,6},{6,7},{7,4},{8,9},{9,10},{10,1... | collective-permute-start | bytes 786440 | tf_op jit(solution)/shard_map/ppermute | solution.py:474
  240.3 6.9 %collective-permute-start.14 = (bf16[256,512]{1,0:T(8,128)(2,1)S(1)}, bf16[256,512]{1,0:T(8,128)(2,1)S(1)}, u32[]{:S(2)}, u32[]{:S(2)}) collective-permute-start(bf16[256,512]{1,0:T(8,128)(2,1)S(1)} %slice.29), channel_id=1, source_target_pairs={{0,3},{1,0},{2,1},{3,2},{4,7},{5,4},{6,5},{7,6},{8,11},{9,8},{10,9... | collective-permute-start | bytes 786440 | tf_op jit(solution)/shard_map/ppermute | solution.py:475
  (9 other events, 15.8 us)

commit v4 on v3

--- a/solution.py
+++ b/solution.py
@@ -491,11 +491,14 @@
     for h in range(CHUNKS):
         own = arrived[h]
         mid = own.shape[0] // 2
-        left = lax.ppermute(own, "tile", RIGHT)
-        right = lax.ppermute(own, "tile", LEFT)
-        opposite = [lax.ppermute(left[0:mid], "tile", RIGHT), lax.ppermute(right[mid:], "tile", LEFT)]
+        fore = own[0:mid], own[mid:]
+        left_fore = lax.ppermute(fore[0], "tile", RIGHT)
+        right_fore = lax.ppermute(fore[1], "tile", LEFT)
+        left_aft = lax.ppermute(fore[1], "tile", RIGHT)
+        right_aft = lax.ppermute(fore[0], "tile", LEFT)
+        opposite = [lax.ppermute(left_fore, "tile", RIGHT), lax.ppermute(right_fore, "tile", LEFT)]
         form("own", h, (0,), ([own],))
-        form("side", h, (1, 3), ([right], [left]))
+        form("side", h, (1, 3), ([right_aft, right_fore], [left_fore, left_aft]))
         if h + 1 < CHUNKS:
             form("far", h, (2,), (opposite,))
     crossed = cross(CHUNKS - 1, me, recv, places, recoup, pieces, opposite, codes["far"])

time: 281 us -> 279 us (level)
  waiting for transfers between devices: 126 us -> 117 us
  starting transfers between devices: 51.7 us -> 60 us
    ppermute x1, waiting for transfers between devices: 19.3 us -> 2.56 us  [on_device(): lax.ppermute(recv, 'tile', RIGHT)]
    ppermute x1, waiting for transfers between devices: 1.3 us -> 10.2 us  [on_device(): lax.ppermute(recv, 'tile', LEFT)]
    slice x4 -> x2, local copies, waits for them, and re-layouts: 4.67 us -> 1.15 us  [on_device(): fore = (own[0:mid], own[mid:])]
    all_to_all x1, starting transfers between devices: 13.8 us -> 17.2 us  [on_device(): lax.all_to_all(crossed, 'chan', split_axis=0, concat_axis=0, tiled=True)]
    ppermute x8 -> x12, starting transfers between devices: 9.69 us -> 12.9 us  [the longest x2 4.26 us: on_device(): right_fore = lax.ppermute(fore[1], 'tile', LEFT)]
    unnamed x30 -> x38, local copies, waits for them, and re-layouts: 3.79 us -> 5.87 us
    ppermute x8 -> x12, waiting for transfers between devices: 17.9 us -> 18.8 us  [the longest x2 18.8 us: on_device(): left_aft = lax.ppermute(fore[1], 'tile', RIGHT)]
  transfers between devices with their start and end apart: 18 -> 22, of which waited for: 9 -> 9; matrix products, arithmetic and copies ran while one was open for 2% -> 0% of each run, Pallas kernels for 23% -> 23%
where the time goes in v4:
time: 279 us; the launch traced here: 277 us
  waiting for transfers between devices  117 us (42%)
  Pallas kernels  92.6 us (33%)
  starting transfers between devices  60 us (22%)
  local copies, waits for them, and re-layouts  7.06 us (3%)
    all_to_all x2, waiting for transfers between devices, on_device(): lax.all_to_all(buf, 'chan', split_axis=0, concat_axis=0, tiled=True)  51.3 us
    ppermute x1, waiting for transfers between devices, on_device(): from_left = lax.ppermute(to_right, 'tile', RIGHT)  28.6 us
    pallas_call x5, Pallas kernels, recouple(): pl.pallas_call(functools.partial(recouple_kernel, chunk, across, parts, b...  28.3 us
    pallas_call x1, Pallas kernels, ladder_base(): pl.pallas_call(functools.partial(ladder_kernel, step_size), out_shape=jax...  25.4 us
    pallas_call x1, Pallas kernels, cross(): pl.pallas_call(functools.partial(cross_kernel, chunk, blocks, len(raws)),...  19.6 us
    all_to_all x2, starting transfers between devices, on_device(): lax.all_to_all(buf, 'chan', split_axis=0, concat_axis=0, tiled=True)  19.2 us
    ppermute x2, waiting for transfers between devices, on_device(): left_aft = lax.ppermute(fore[1], 'tile', RIGHT)  18.8 us
    all_to_all x1, starting transfers between devices, on_device(): lax.all_to_all(crossed, 'chan', split_axis=0, concat_axis=0, tiled=True)  17.2 us
  transfers between devices with their start and end apart: 22, of which 9 were waited for; matrix products, arithmetic and copies ran while one was open for 0% of the time, Pallas kernels for 23%

profile of v4, /device:TPU:1, one launch (start us, length us, event | category | flops | bytes accessed | tf_op | source)
XLA Modules:
  0.0 277.1 jit_solution(16055335502553631603)
XLA Ops:
  0.0 3.5 %shard_map.77 = bf16[64,64,128]{2,1,0:T(8,128)(2,1)} custom-call(s32[1]{0:T(128)} %bitcast.2.me, s32[4,16]{1,0:T(4,128)} %bitcast.10, s32[4,16]{1,0:T(4,128)} %bitcast.13, bf16[512,2048]{1,0:T(8,128)(2,1)} %bitcast.6, f32[1,2048]{1,0:T(1,128)} %energy.5, s32[1,2048]{1,0:T(1,128)} %occ.5), custom_call_target="tpu_custom_call" | custom-call | tf_op jit(solution)/shard_map/pallas_call | solution.py:60
  3.5 13.0 %all-to-all-start.1 = ((bf16[64,64,128]{2,1,0:T(8,128)(2,1)}), bf16[64,64,128]{2,1,0:T(8,128)(2,1)S(1)}, u32[]{:S(2)}, u32[]{:S(2)}) async-start(bf16[64,64,128]{2,1,0:T(8,128)(2,1)} %shard_map.77), calls=%async_computation.1 | async-start | bytes 2097152 | tf_op jit(solution)/shard_map/all_to_all | solution.py:469
  16.4 3.7 %shard_map.73 = bf16[64,72,128]{2,1,0:T(8,128)(2,1)} custom-call(s32[1]{0:T(128)} %bitcast.2.me, s32[4,16]{1,0:T(4,128)} %bitcast.11, s32[4,16]{1,0:T(4,128)} %bitcast.14, bf16[512,2048]{1,0:T(8,128)(2,1)} %bitcast.7, f32[1,2048]{1,0:T(1,128)} %energy.5, s32[1,2048]{1,0:T(1,128)} %occ.5), custom_call_target="tpu_custom_call" | custom-call | tf_op jit(solution)/shard_map/pallas_call | solution.py:60
  20.1 24.5 %all-to-all-done.1.refs_0_ = bf16[64,64,128]{2,1,0:T(8,128)(2,1)S(1)} async-done(((bf16[64,64,128]{2,1,0:T(8,128)(2,1)}), bf16[64,64,128]{2,1,0:T(8,128)(2,1)S(1)}, u32[]{:S(2)}, u32[]{:S(2)}) %all-to-all-start.1) | async-done | bytes 1048608 | tf_op jit(solution)/shard_map/all_to_all | solution.py:469
  44.6 6.3 %all-to-all-start = ((bf16[64,72,128]{2,1,0:T(8,128)(2,1)}), bf16[64,72,128]{2,1,0:T(8,128)(2,1)S(1)}, u32[]{:S(2)}, u32[]{:S(2)}) async-start(bf16[64,72,128]{2,1,0:T(8,128)(2,1)} %shard_map.73), calls=%async_computation | async-start | bytes 2359296 | tf_op jit(solution)/shard_map/all_to_all | solution.py:469
  52.0 2.7 collective-permute-start.10
  54.7 26.8 %all-to-all-done.refs_0_ = bf16[64,72,128]{2,1,0:T(8,128)(2,1)S(1)} async-done(((bf16[64,72,128]{2,1,0:T(8,128)(2,1)}), bf16[64,72,128]{2,1,0:T(8,128)(2,1)S(1)}, u32[]{:S(2)}, u32[]{:S(2)}) %all-to-all-start) | async-done | bytes 1179680 | tf_op jit(solution)/shard_map/all_to_all | solution.py:469
  85.9 10.2 %collective-permute-done.right = s32[4,16]{1,0:T(4,128)S(1)} collective-permute-done((s32[4,16]{1,0:T(4,128)S(1)}, s32[4,16]{1,0:T(4,128)S(1)}, u32[]{:S(2)}, u32[]{:S(2)}) %collective-permute-start) | collective-permute-done | bytes 288 | tf_op jit(solution)/shard_map/ppermute | solution.py:478
  96.1 2.6 collective-permute-start.1
  106.8 2.7 collective-permute-start.6
  109.4 18.8 %collective-permute-done.12.refs_3_ = bf16[32,64,128]{2,1,0:T(8,128)(2,1)S(1)} collective-permute-done((bf16[32,64,128]{2,1,0:T(8,128)(2,1)}, bf16[32,64,128]{2,1,0:T(8,128)(2,1)S(1)}, u32[]{:S(2)}, u32[]{:S(2)}) %collective-permute-start.12) | collective-permute-done | bytes 524320 | tf_op jit(solution)/shard_map/ppermute | solution.py:497
  131.8 3.7 %place_tables.1.places = s32[4,64]{1,0:T(4,128)} custom-call(s32[4,16]{1,0:T(4,128)} %bitcast.16, s32[4,16]{1,0:T(4,128)} %copy-done.16, s32[4,16]{1,0:T(4,128)} %copy-done.17, s32[4,16]{1,0:T(4,128)} %copy-done.18), custom_call_target="tpu_custom_call" | custom-call | tf_op jit(solution)/shard_map/place_tables/pallas_call | solution.py:81
  135.5 5.0 %shard_map.75 = (bf16[4,64,2048]{2,1,0:T(8,128)(2,1)}, bf16[4,64,2048]{2,1,0:T(8,128)(2,1)}, f32[1,128,128]{2,1,0:T(8,128)}, f32[1,64,128]{2,1,0:T(8,128)}, s32[1,8,128]{2,1,0:T(8,128)}) custom-call(s32[4,64]{1,0:T(4,128)} %place_tables.1.places, bf16[8,128,128]{2,1,0:T(8,128)(2,1)} %recoup.13, bf16[64,72,128]{2,1,0:T(8,128)(2,1)} %copy-done), custom_call_target="tpu_custom_call" | custom-call | tf_op jit(solution)/shard_map/pallas_call | solution.py:305
  140.5 4.5 %shard_map.78 = (bf16[4,64,2048]{2,1,0:T(8,128)(2,1)}, bf16[4,64,2048]{2,1,0:T(8,128)(2,1)}) custom-call(s32[4,64]{1,0:T(4,128)} %place_tables.1.places, bf16[8,128,128]{2,1,0:T(8,128)(2,1)} %recoup.13, bf16[64,64,128]{2,1,0:T(8,128)(2,1)} %copy-done.1, f32[1,128,128]{2,1,0:T(8,128)} %get-tuple-element.35.refs_1_, f32[1,64,128]{2,1,0:T(8,128)} %get-tuple-element.36.refs_2_, ...), custom_call_target="tpu_custom_call" | custom-call | tf_op jit(solution)/shard_map/pallas_call | solution.py:305
  145.1 7.4 %shard_map.76 = (bf16[8,64,2048]{2,1,0:T(8,128)(2,1)}, bf16[8,64,2048]{2,1,0:T(8,128)(2,1)}, f32[2,128,128]{2,1,0:T(8,128)}, f32[2,64,128]{2,1,0:T(8,128)}, s32[2,8,128]{2,1,0:T(8,128)}) custom-call(s32[4,64]{1,0:T(4,128)} %place_tables.1.places, bf16[8,128,128]{2,1,0:T(8,128)(2,1)} %recoup.13, bf16[32,72,128]{2,1,0:T(8,128)(2,1)} %copy-done.8, ...), custom_call_target="tpu_custom_call" | custom-call | tf_op jit(solution)/shard_map/pallas_call | solution.py:305
  152.5 6.4 %shard_map.79 = (bf16[8,64,2048]{2,1,0:T(8,128)(2,1)}, bf16[8,64,2048]{2,1,0:T(8,128)(2,1)}) custom-call(s32[4,64]{1,0:T(4,128)} %place_tables.1.places, bf16[8,128,128]{2,1,0:T(8,128)(2,1)} %recoup.13, bf16[32,64,128]{2,1,0:T(8,128)(2,1)} %collective-permute-done.9.refs_0_, bf16[32,64,128]{2,1,0:T(8,128)(2,1)} %copy-done.10, ...), custom_call_target="tpu_custom_call" | custom-call | tf_op jit(solution)/shard_map/pallas_call | solution.py:305
  160.5 5.1 %shard_map.74 = (bf16[4,64,2048]{2,1,0:T(8,128)(2,1)}, bf16[4,64,2048]{2,1,0:T(8,128)(2,1)}, f32[1,128,128]{2,1,0:T(8,128)}, f32[1,64,128]{2,1,0:T(8,128)}, s32[1,8,128]{2,1,0:T(8,128)}) custom-call(s32[4,64]{1,0:T(4,128)} %place_tables.1.places, bf16[8,128,128]{2,1,0:T(8,128)(2,1)} %recoup.13, bf16[32,72,128]{2,1,0:T(8,128)(2,1)} %copy-done.4, ...), custom_call_target="tpu_custom_call" | custom-call | tf_op jit(solution)/shard_map/pallas_call | solution.py:305
  165.6 19.6 %cross.1 = bf16[64,128,128]{2,1,0:T(8,128)(2,1)} custom-call(s32[1]{0:T(128)} %bitcast.2.me, s32[4,16]{1,0:T(4,128)} %bitcast.17, s32[4,64]{1,0:T(4,128)} %place_tables.1.places, s32[1,8,128]{2,1,0:T(8,128)} %get-tuple-element.26.cls, bf16[8,128,128]{2,1,0:T(8,128)(2,1)} %recoup.13, f32[1,128,128]{2,1,0:T(8,128)} %get-tuple-element.27.down, ...), custom_call_target="tpu_custom_call" | custom-call | tf_op jit(solution)/shard_map/cross/pallas_call | solution.py:395
  185.2 17.2 %all-to-all-start.2 = ((bf16[64,128,128]{2,1,0:T(8,128)(2,1)}), bf16[64,128,128]{2,1,0:T(8,128)(2,1)S(1)}, u32[]{:S(2)}, u32[]{:S(2)}) async-start(bf16[64,128,128]{2,1,0:T(8,128)(2,1)} %cross.1), calls=%async_computation.2 | async-start | bytes 4194304 | tf_op jit(solution)/shard_map/all_to_all | solution.py:505
  202.5 3.3 %share_blocks.1 = (bf16[1280,512]{1,0:T(8,128)(2,1)}, bf16[1280,512]{1,0:T(8,128)(2,1)}) custom-call(s32[1]{0:T(128)} %bitcast.2.me, bf16[512,2048]{1,0:T(8,128)(2,1)} %bitcast.8), custom_call_target="tpu_custom_call" | custom-call | tf_op jit(solution)/shard_map/share_blocks/pallas_call | solution.py:111
  208.5 28.6 %collective-permute-done.15.from_left = bf16[1280,512]{1,0:T(8,128)(2,1)S(1)} collective-permute-done((bf16[1280,512]{1,0:T(8,128)(2,1)}, bf16[1280,512]{1,0:T(8,128)(2,1)S(1)}, u32[]{:S(2)}, u32[]{:S(2)}) %collective-permute-start.15) | collective-permute-done | bytes 1310752 | tf_op jit(solution)/shard_map/ppermute | solution.py:472
  241.0 3.9 %collective-permute-done.17.far_a = bf16[256,512]{1,0:T(8,128)(2,1)S(1)} collective-permute-done((bf16[256,512]{1,0:T(8,128)(2,1)S(1)}, bf16[256,512]{1,0:T(8,128)(2,1)S(1)}, u32[]{:S(2)}, u32[]{:S(2)}) %collective-permute-start.17) | collective-permute-done | bytes 262176 | tf_op jit(solution)/shard_map/ppermute | solution.py:474
  246.4 25.4 %ladder.1.base = f32[512,2048]{1,0:T(8,128)} custom-call(s32[1]{0:T(128)} %bitcast.2.me, bf16[512,2048]{1,0:T(8,128)(2,1)} %bitcast.9, bf16[1280,512]{1,0:T(8,128)(2,1)} %copy-done.2, bf16[1280,512]{1,0:T(8,128)(2,1)} %copy-done.3, bf16[256,512]{1,0:T(8,128)(2,1)} %copy-done.13, bf16[256,512]{1,0:T(8,128)(2,1)} %copy-done.14, f32[1,2048]{1,0:T(1,128)} %energy.5, ...), custom_call_target="tpu_custom_call" | custom-call | tf_op jit(solution)/shard_map/ladder/pallas_call | solution.py:177
  271.8 5.1 %finish.1 = f32[512,2048]{1,0:T(8,128)} custom-call(s32[4,16]{1,0:T(4,128)} %bitcast.12, s32[4,16]{1,0:T(4,128)} %bitcast.15, bf16[8,128,128]{2,1,0:T(8,128)(2,1)} %recoup.13, bf16[64,128,128]{2,1,0:T(8,128)(2,1)S(1)} %all-to-all-done.2.tiles, f32[512,2048]{1,0:T(8,128)} %ladder.1.base), custom_call_target="tpu_custom_call" | custom-call | tf_op jit(solution)/shard_map/finish/pallas_call | solution.py:438
  (74 shorter events, 26.7 us)
Async XLA Ops:
  3.5 41.1 %all-to-all-start.1 = ((bf16[64,64,128]{2,1,0:T(8,128)(2,1)}), bf16[64,64,128]{2,1,0:T(8,128)(2,1)S(1)}, u32[]{:S(2)}, u32[]{:S(2)}) async-start(bf16[64,64,128]{2,1,0:T(8,128)(2,1)} %shard_map.77), calls=%async_computation.1 | async-start | bytes 2097152 | tf_op jit(solution)/shard_map/all_to_all | solution.py:469
  44.6 36.9 %all-to-all-start = ((bf16[64,72,128]{2,1,0:T(8,128)(2,1)}), bf16[64,72,128]{2,1,0:T(8,128)(2,1)S(1)}, u32[]{:S(2)}, u32[]{:S(2)}) async-start(bf16[64,72,128]{2,1,0:T(8,128)(2,1)} %shard_map.73), calls=%async_computation | async-start | bytes 2359296 | tf_op jit(solution)/shard_map/all_to_all | solution.py:469
  52.0 53.7 %collective-permute-start.10 = (bf16[32,64,128]{2,1,0:T(8,128)(2,1)}, bf16[32,64,128]{2,1,0:T(8,128)(2,1)S(1)}, u32[]{:S(2)}, u32[]{:S(2)}) collective-permute-start(bf16[32,64,128]{2,1,0:T(8,128)(2,1)} %get-tuple-element.49), channel_id=1, source_target_pairs={{0,3},{1,0},{2,1},{3,2},{4,7},{5,4},{6,5},{7,6},{8,11},{9,8},{10,9... | collective-permute-start | bytes 1572872 | tf_op jit(solution)/shard_map/ppermute | solution.py:496
  54.7 51.0 %collective-permute-start.11 = (bf16[32,64,128]{2,1,0:T(8,128)(2,1)}, bf16[32,64,128]{2,1,0:T(8,128)(2,1)S(1)}, u32[]{:S(2)}, u32[]{:S(2)}) collective-permute-start(bf16[32,64,128]{2,1,0:T(8,128)(2,1)} %get-tuple-element.50), channel_id=1, source_target_pairs={{0,1},{1,2},{2,3},{3,0},{4,5},{5,6},{6,7},{7,4},{8,9},{9,10},{10,1... | collective-permute-start | bytes 1572872 | tf_op jit(solution)/shard_map/ppermute | solution.py:495
  81.5 54.0 %copy-start = (bf16[64,72,128]{2,1,0:T(8,128)(2,1)}, bf16[64,72,128]{2,1,0:T(8,128)(2,1)S(1)}, u32[]{:S(2)}) copy-start(bf16[64,72,128]{2,1,0:T(8,128)(2,1)S(1)} %all-to-all-done.refs_0_) | copy-start | bytes 3538948
  81.6 25.1 %collective-permute-start.3 = (bf16[32,72,128]{2,1,0:T(8,128)(2,1)S(1)}, bf16[32,72,128]{2,1,0:T(8,128)(2,1)S(1)}, u32[]{:S(2)}, u32[]{:S(2)}) collective-permute-start(bf16[32,72,128]{2,1,0:T(8,128)(2,1)S(1)} %get-tuple-element.48), channel_id=1, source_target_pairs={{0,1},{1,2},{2,3},{3,0},{4,5},{5,6},{6,7},{7,4},{8,9},{9,10},{10,1... | collective-permute-start | bytes 1769480 | tf_op jit(solution)/shard_map/ppermute | solution.py:495
  83.0 23.8 %collective-permute-start.5 = (bf16[32,72,128]{2,1,0:T(8,128)(2,1)S(1)}, bf16[32,72,128]{2,1,0:T(8,128)(2,1)S(1)}, u32[]{:S(2)}, u32[]{:S(2)}) collective-permute-start(bf16[32,72,128]{2,1,0:T(8,128)(2,1)S(1)} %get-tuple-element.47), channel_id=1, source_target_pairs={{0,3},{1,0},{2,1},{3,2},{4,7},{5,4},{6,5},{7,6},{8,11},{9,8},{10,9... | collective-permute-start | bytes 1769480 | tf_op jit(solution)/shard_map/ppermute | solution.py:496
  84.5 11.6 %collective-permute-start = (s32[4,16]{1,0:T(4,128)S(1)}, s32[4,16]{1,0:T(4,128)S(1)}, u32[]{:S(2)}, u32[]{:S(2)}) collective-permute-start(s32[4,16]{1,0:T(4,128)S(1)} %bitcast.18), channel_id=1, source_target_pairs={{0,3},{1,0},{2,1},{3,2},{4,7},{5,4},{6,5},{7,6},{8,11},{9,8},{10,9... | collective-permute-start | bytes 776 | tf_op jit(solution)/shard_map/ppermute | solution.py:478
  96.1 3.9 %collective-permute-start.1 = (s32[4,16]{1,0:T(4,128)S(1)}, s32[4,16]{1,0:T(4,128)S(1)}, u32[]{:S(2)}, u32[]{:S(2)}) collective-permute-start(s32[4,16]{1,0:T(4,128)S(1)} %bitcast.19), channel_id=1, source_target_pairs={{0,2},{1,3},{2,0},{3,1},{4,6},{5,7},{6,4},{7,5},{8,10},{9,11},{10,... | collective-permute-start | bytes 776 | tf_op jit(solution)/shard_map/ppermute | solution.py:479
  100.1 3.9 %collective-permute-start.2 = (s32[4,16]{1,0:T(4,128)S(1)}, s32[4,16]{1,0:T(4,128)S(1)}, u32[]{:S(2)}, u32[]{:S(2)}) collective-permute-start(s32[4,16]{1,0:T(4,128)S(1)} %bitcast.20), channel_id=1, source_target_pairs={{0,1},{1,2},{2,3},{3,0},{4,5},{5,6},{6,7},{7,4},{8,9},{9,10},{10,1... | collective-permute-start | bytes 776 | tf_op jit(solution)/shard_map/ppermute | solution.py:480
  103.9 24.3 %collective-permute-start.7 = (bf16[32,72,128]{2,1,0:T(8,128)(2,1)S(1)}, bf16[32,72,128]{2,1,0:T(8,128)(2,1)S(1)}, u32[]{:S(2)}, u32[]{:S(2)}) collective-permute-start(bf16[32,72,128]{2,1,0:T(8,128)(2,1)S(1)} %get-tuple-element.48), channel_id=1, source_target_pairs={{0,3},{1,0},{2,1},{3,2},{4,7},{5,4},{6,5},{7,6},{8,11},{9,8},{10,9... | collective-permute-start | bytes 1769480 | tf_op jit(solution)/shard_map/ppermute | solution.py:498
  105.7 24.0 %collective-permute-start.8 = (bf16[32,72,128]{2,1,0:T(8,128)(2,1)S(1)}, bf16[32,72,128]{2,1,0:T(8,128)(2,1)S(1)}, u32[]{:S(2)}, u32[]{:S(2)}) collective-permute-start(bf16[32,72,128]{2,1,0:T(8,128)(2,1)S(1)} %get-tuple-element.47), channel_id=1, source_target_pairs={{0,1},{1,2},{2,3},{3,0},{4,5},{5,6},{6,7},{7,4},{8,9},{9,10},{10,1... | collective-permute-start | bytes 1769480 | tf_op jit(solution)/shard_map/ppermute | solution.py:497
  105.7 22.5 %collective-permute-start.12 = (bf16[32,64,128]{2,1,0:T(8,128)(2,1)}, bf16[32,64,128]{2,1,0:T(8,128)(2,1)S(1)}, u32[]{:S(2)}, u32[]{:S(2)}) collective-permute-start(bf16[32,64,128]{2,1,0:T(8,128)(2,1)} %get-tuple-element.49), channel_id=1, source_target_pairs={{0,1},{1,2},{2,3},{3,0},{4,5},{5,6},{6,7},{7,4},{8,9},{9,10},{10,1... | collective-permute-start | bytes 1572872 | tf_op jit(solution)/shard_map/ppermute | solution.py:497
  106.7 38.3 %copy-start.6 = (bf16[32,72,128]{2,1,0:T(8,128)(2,1)}, bf16[32,72,128]{2,1,0:T(8,128)(2,1)S(1)}, u32[]{:S(2)}) copy-start(bf16[32,72,128]{2,1,0:T(8,128)(2,1)S(1)} %collective-permute-done.3.refs_2_) | copy-start | bytes 1769476
  106.7 52.1 %collective-permute-start.4 = (bf16[32,72,128]{2,1,0:T(8,128)(2,1)S(1)}, bf16[32,72,128]{2,1,0:T(8,128)(2,1)S(1)}, u32[]{:S(2)}, u32[]{:S(2)}) collective-permute-start(bf16[32,72,128]{2,1,0:T(8,128)(2,1)S(1)} %collective-permute-done.3.refs_2_), channel_id=1, source_target_pairs={{0,1},{1,2},{2,3},{3,0},{4,5},{5,6},{6,7},{7,4},{8,9},{9,10},{10,1... | collective-permute-start | bytes 1769480 | tf_op jit(solution)/shard_map/ppermute | solution.py:499
  106.8 52.1 %collective-permute-start.6 = (bf16[32,72,128]{2,1,0:T(8,128)(2,1)S(1)}, bf16[32,72,128]{2,1,0:T(8,128)(2,1)S(1)}, u32[]{:S(2)}, u32[]{:S(2)}) collective-permute-start(bf16[32,72,128]{2,1,0:T(8,128)(2,1)S(1)} %collective-permute-done.5.refs_1_), channel_id=1, source_target_pairs={{0,3},{1,0},{2,1},{3,2},{4,7},{5,4},{6,5},{7,6},{8,11},{9,8},{10,9... | collective-permute-start | bytes 1769480 | tf_op jit(solution)/shard_map/ppermute | solution.py:499
  128.2 24.3 %collective-permute-start.9 = (bf16[32,64,128]{2,1,0:T(8,128)(2,1)}, bf16[32,64,128]{2,1,0:T(8,128)(2,1)}, u32[]{:S(2)}, u32[]{:S(2)}) collective-permute-start(bf16[32,64,128]{2,1,0:T(8,128)(2,1)} %get-tuple-element.50), channel_id=1, source_target_pairs={{0,3},{1,0},{2,1},{3,2},{4,7},{5,4},{6,5},{7,6},{8,11},{9,8},{10,9... | collective-permute-start | bytes 1572872 | tf_op jit(solution)/shard_map/ppermute | solution.py:498
  128.2 37.3 %collective-permute-start.13 = (bf16[32,64,128]{2,1,0:T(8,128)(2,1)}, bf16[32,64,128]{2,1,0:T(8,128)(2,1)}, u32[]{:S(2)}, u32[]{:S(2)}) collective-permute-start(bf16[32,64,128]{2,1,0:T(8,128)(2,1)} %copy-done.11), channel_id=1, source_target_pairs={{0,1},{1,2},{2,3},{3,0},{4,5},{5,6},{6,7},{7,4},{8,9},{9,10},{10,1... | collective-permute-start | bytes 1572872 | tf_op jit(solution)/shard_map/ppermute | solution.py:499
  130.5 35.0 %collective-permute-start.14 = (bf16[32,64,128]{2,1,0:T(8,128)(2,1)}, bf16[32,64,128]{2,1,0:T(8,128)(2,1)}, u32[]{:S(2)}, u32[]{:S(2)}) collective-permute-start(bf16[32,64,128]{2,1,0:T(8,128)(2,1)} %copy-done.10), channel_id=1, source_target_pairs={{0,3},{1,0},{2,1},{3,2},{4,7},{5,4},{6,5},{7,6},{8,11},{9,8},{10,9... | collective-permute-start | bytes 1572872 | tf_op jit(solution)/shard_map/ppermute | solution.py:499
  185.2 86.5 %all-to-all-start.2 = ((bf16[64,128,128]{2,1,0:T(8,128)(2,1)}), bf16[64,128,128]{2,1,0:T(8,128)(2,1)S(1)}, u32[]{:S(2)}, u32[]{:S(2)}) async-start(bf16[64,128,128]{2,1,0:T(8,128)(2,1)} %cross.1), calls=%async_computation.2 | async-start | bytes 4194304 | tf_op jit(solution)/shard_map/all_to_all | solution.py:505
  205.8 31.3 %collective-permute-start.15 = (bf16[1280,512]{1,0:T(8,128)(2,1)}, bf16[1280,512]{1,0:T(8,128)(2,1)S(1)}, u32[]{:S(2)}, u32[]{:S(2)}) collective-permute-start(bf16[1280,512]{1,0:T(8,128)(2,1)} %get-tuple-element.45), channel_id=1, source_target_pairs={{0,1},{1,2},{2,3},{3,0},{4,5},{5,6},{6,7},{7,4},{8,9},{9,10},{10,1... | collective-permute-start | bytes 3932168 | tf_op jit(solution)/shard_map/ppermute | solution.py:472
  206.2 31.0 %collective-permute-start.16 = (bf16[1280,512]{1,0:T(8,128)(2,1)}, bf16[1280,512]{1,0:T(8,128)(2,1)S(1)}, u32[]{:S(2)}, u32[]{:S(2)}) collective-permute-start(bf16[1280,512]{1,0:T(8,128)(2,1)} %get-tuple-element.46), channel_id=1, source_target_pairs={{0,3},{1,0},{2,1},{3,2},{4,7},{5,4},{6,5},{7,6},{8,11},{9,8},{10,9... | collective-permute-start | bytes 3932168 | tf_op jit(solution)/shard_map/ppermute | solution.py:473
  237.1 7.8 %collective-permute-start.17 = (bf16[256,512]{1,0:T(8,128)(2,1)S(1)}, bf16[256,512]{1,0:T(8,128)(2,1)S(1)}, u32[]{:S(2)}, u32[]{:S(2)}) collective-permute-start(bf16[256,512]{1,0:T(8,128)(2,1)S(1)} %slice.28), channel_id=1, source_target_pairs={{0,1},{1,2},{2,3},{3,0},{4,5},{5,6},{6,7},{7,4},{8,9},{9,10},{10,1... | collective-permute-start | bytes 786440 | tf_op jit(solution)/shard_map/ppermute | solution.py:474
  238.4 6.7 %collective-permute-start.18 = (bf16[256,512]{1,0:T(8,128)(2,1)S(1)}, bf16[256,512]{1,0:T(8,128)(2,1)S(1)}, u32[]{:S(2)}, u32[]{:S(2)}) collective-permute-start(bf16[256,512]{1,0:T(8,128)(2,1)S(1)} %slice.29), channel_id=1, source_target_pairs={{0,3},{1,0},{2,1},{3,2},{4,7},{5,4},{6,5},{7,6},{8,11},{9,8},{10,9... | collective-permute-start | bytes 786440 | tf_op jit(solution)/shard_map/ppermute | solution.py:475
  (17 other events, 192.7 us)
